TPU v7x, 32 devices: a whole 2x2x4 slice. The times are simulated.
32 devices in a mesh: sample: 4 (over x, core), ctx: 8 (over z, y).
Axes of the slice: x: 2, y: 2, z: 4, core: 2. Of those that a mesh axis runs over, the one named last changes fastest.
Arguments:
- queries: bfloat16 [4096, 2048], P(('sample', 'ctx')), may hold values from -4 to 4
- experts: int32 [4096, 16], P(('sample', 'ctx')), may hold values from 0 to 63, all different within a row; in each aligned block of 128 rows (0 to 127, 128 to 255, ...) at most 64 rows name the same one
- gate: float32 [4096, 16], P(('sample', 'ctx')), may hold values from 0.05 to 1
- prefix_keys: bfloat16 [128, 1024], P('ctx'), may hold values from -8 to 8
- prefix_values: bfloat16 [128, 1024], P('ctx'), may hold values from -6 to 6
- d_out: bfloat16 [4096, 2048], P(('sample', 'ctx')), may hold values from -6 to 6
- lengths: int32 [4], replicated, may hold values from 128 to 1024
Outputs:
- attended: bfloat16 [4096, 2048], P(('sample', 'ctx'))
- query_grad: bfloat16 [4096, 2048], P(('sample', 'ctx'))
- gate_grad: float32 [4096, 16], P(('sample', 'ctx'))
- key_grad: float32 [128, 1024], P('ctx')
- value_grad: float32 [128, 1024], P('ctx')
Inputs may be any that keep to these rules, and one draw needn't show every extreme that they name: `experts`: among the tokens of one device (aligned blocks of 128 tokens) no expert is picked more than 64 times, and some expert is picked exactly 64 times; a token's picks are distinct. Completion c holds tokens c * 1024 to (c + 1) * 1024 - 1; its first lengths[c] tokens are live.
All inputs are finite; a program needn't handle non-finite values.
Results may differ from a plain program's by a relative error of at most 0.012.
Values may be sent and summed in bfloat16 or wider, within the bound.
No kernel may reach another device: no remote copies, remote signals or barrier semaphores. Data moves between devices by JAX's collectives and lax.ppermute only.
A program may use at most 64 MiB of HBM per device.

v0:
```python
import jax
import jax.numpy as jnp
from jax import lax
from jax.sharding import PartitionSpec as P

HEAD = 128
KV_HEADS = 8
EXPERTS = 64
TOPK = 16
CLEN = 1024
CAP = 64


def slot_index(experts):
    flat = experts.reshape(-1)
    picked = (flat[:, None] == jnp.arange(EXPERTS, dtype=jnp.int32)[None, :]).astype(jnp.int32)
    before = jnp.cumsum(picked, axis=0) - picked
    return flat * CAP + jnp.sum(before * picked, axis=1)


def over_blocks(step, carry, pieces, start):
    keys, values = pieces
    length = keys.shape[0]
    if length > 128 and length % 128 == 0:

        def inner(state, number):
            begin = number * 128
            key_block = lax.dynamic_slice_in_dim(keys, begin, 128, 0)
            value_block = lax.dynamic_slice_in_dim(values, begin, 128, 0)
            return (step(state, key_block, value_block, start + begin), None)

        carry, _ = lax.scan(inner, carry, jnp.arange(length // 128, dtype=jnp.int32))
        return carry
    return step(carry, keys, values, start)


def local(queries, experts, gate, prefix_keys, prefix_values, d_out, lengths):
    scale = HEAD ** (-0.5)
    width = KV_HEADS * HEAD
    group = EXPERTS * CAP // KV_HEADS
    rows = queries.shape[0]
    n_ctx = lax.axis_size("ctx")
    prefix_total = prefix_keys.shape[0] * n_ctx
    block = lax.axis_index("sample") * n_ctx + lax.axis_index("ctx")
    token_ids = block * rows + jnp.arange(rows, dtype=jnp.int32)
    owners = (token_ids // CLEN)[:, None] == jnp.arange(lengths.shape[0], dtype=jnp.int32)[None, :]
    chosen = jnp.sum(jnp.where(owners, lengths[None, :], 0), axis=1)
    live = (token_ids % CLEN < chosen).astype(jnp.float32)
    slots = slot_index(experts)
    q_buf = jnp.zeros((EXPERTS * CAP, HEAD), jnp.bfloat16).at[slots].set(queries.reshape(-1, HEAD))
    q_buf = q_buf.reshape(KV_HEADS, group, HEAD)

    def scores_of(key_block):
        heads = key_block.reshape(-1, KV_HEADS, HEAD)
        return jnp.einsum("hgd,phd->hgp", q_buf, heads, preferred_element_type=jnp.float32) * scale

    def forward_step(carry, key_block, value_block, start):
        high, total, accum = carry
        score = scores_of(key_block)
        new_high = jnp.maximum(high, jnp.max(score, axis=2))
        shrink = jnp.exp(high - new_high)
        weight = jnp.exp(score - new_high[..., None])
        total = total * shrink + jnp.sum(weight, axis=2)
        heads = value_block.reshape(-1, KV_HEADS, HEAD)
        accum = accum * shrink[..., None] + jnp.einsum(
            "hgp,phd->hgd", weight.astype(jnp.bfloat16), heads, preferred_element_type=jnp.float32
        )
        return (new_high, total, accum)

    start_state = (
        jnp.full((KV_HEADS, group), -1e30, jnp.float32),
        jnp.zeros((KV_HEADS, group), jnp.float32),
        jnp.zeros((KV_HEADS, group, HEAD), jnp.float32),
    )
    high, total, accum = over_blocks(
        forward_step,
        start_state,
        (
            lax.all_gather(prefix_keys, "ctx", axis=0, tiled=True),
            lax.all_gather(prefix_values, "ctx", axis=0, tiled=True),
        ),
        jnp.int32(0),
    )
    output = accum / total[..., None]
    lse = high + jnp.log(total)
    o_rows = output.reshape(EXPERTS * CAP, HEAD)[slots].reshape(rows, TOPK, HEAD)
    cot = d_out.astype(jnp.float32).reshape(rows, TOPK, HEAD)
    factor = gate * live[:, None]
    attended = (factor[..., None] * o_rows).reshape(rows, TOPK * HEAD).astype(jnp.bfloat16)
    gate_grad = live[:, None] * jnp.sum(o_rows * cot, axis=2)
    dout_rows = (factor[..., None] * cot).astype(jnp.bfloat16)
    dout_buf = (
        jnp.zeros((EXPERTS * CAP, HEAD), jnp.bfloat16).at[slots].set(dout_rows.reshape(-1, HEAD))
    )
    dout_buf = dout_buf.reshape(KV_HEADS, group, HEAD)
    delta = jnp.sum(dout_buf.astype(jnp.float32) * output, axis=2)

    def backward_step(carry, key_block, value_block, start):
        dq_accum, grads = carry
        key_heads = key_block.reshape(-1, KV_HEADS, HEAD)
        value_heads = value_block.reshape(-1, KV_HEADS, HEAD)
        prob = jnp.exp(scores_of(key_block) - lse[..., None])
        dprob = jnp.einsum(
            "hgd,phd->hgp", dout_buf, value_heads, preferred_element_type=jnp.float32
        )
        dscore = (prob * (dprob - delta[..., None])).astype(jnp.bfloat16)
        dq_accum = (
            dq_accum
            + jnp.einsum("hgp,phd->hgd", dscore, key_heads, preferred_element_type=jnp.float32)
            * scale
        )
        key_part = (
            jnp.einsum("hgp,hgd->phd", dscore, q_buf, preferred_element_type=jnp.float32) * scale
        )
        value_part = jnp.einsum(
            "hgp,hgd->phd", prob.astype(jnp.bfloat16), dout_buf, preferred_element_type=jnp.float32
        )
        joined = jnp.concatenate(
            [key_part.reshape(-1, width), value_part.reshape(-1, width)], axis=1
        )
        grads = lax.dynamic_update_slice_in_dim(grads, joined, start, 0)
        return (dq_accum, grads)

    back_state = (
        jnp.zeros((KV_HEADS, group, HEAD), jnp.float32),
        jnp.zeros((prefix_total, 2 * width), jnp.float32),
    )
    dq_buf, grads = over_blocks(
        backward_step,
        back_state,
        (
            lax.all_gather(prefix_keys, "ctx", axis=0, tiled=True),
            lax.all_gather(prefix_values, "ctx", axis=0, tiled=True),
        ),
        jnp.int32(0),
    )
    query_grad = (
        dq_buf.reshape(EXPERTS * CAP, HEAD)[slots].reshape(rows, TOPK * HEAD).astype(jnp.bfloat16)
    )
    share = lax.psum_scatter(grads, "ctx", scatter_dimension=0, tiled=True)
    summed = lax.psum(share, "sample")
    return (attended, query_grad, gate_grad, summed[:, :width], summed[:, width:])


def solution(mesh):
    placed = (
        P(("sample", "ctx"), None),
        P(("sample", "ctx"), None),
        P(("sample", "ctx"), None),
        P("ctx", None),
        P("ctx", None),
        P(("sample", "ctx"), None),
        P(),
    )
    return jax.shard_map(
        local,
        mesh=mesh,
        in_specs=placed,
        out_specs=(
            P(("sample", "ctx"), None),
            P(("sample", "ctx"), None),
            P(("sample", "ctx"), None),
            P("ctx", None),
            P("ctx", None),
        ),
        check_vma=False,
    )
```

profile of v0, /device:TPU:0, one launch (start us, length us, event | category | flops | bytes accessed | tf_op | source)
XLA Modules:
  0.0 241.1 jit_solution(4302260018361914511)
XLA Ops:
  7.2 0.0 reduce-scatter.2.cloned.1.call-start
  7.2 0.7 broadcast_multiply_fusion.2
  7.9 0.8 copy.73
  8.7 0.1 eq.47
  8.8 0.1 eq.43
  8.9 0.7 select_reduce_fusion
  9.6 0.6 compare_convert_fusion
  10.2 0.1 copy.72
  10.3 0.1 mul.100
  10.4 1.4 copy.71
  11.8 32.8 %all_gather.8 = bf16[128,1024]{1,0:T(8,128)(2,1)S(1)} all-gather(bf16[16,1024]{1,0:T(8,128)(2,1)} %param.10), channel_id=1, replica_groups=mesh['sample'=4,'ctx'=8] {'ctx'}, dimensions={0}, use_global_device_ids=true | all-gather | bytes 294912 | tf_op jit(solution)/shard_map/all_gather | solution.py:79
  44.6 0.2 copy.77
  44.7 31.0 %all_gather.9 = bf16[128,1024]{1,0:T(8,128)(2,1)S(1)} all-gather(bf16[16,1024]{1,0:T(8,128)(2,1)} %param.11), channel_id=1, replica_groups=mesh['sample'=4,'ctx'=8] {'ctx'}, dimensions={0}, use_global_device_ids=true | all-gather | bytes 294912 | tf_op jit(solution)/shard_map/all_gather | solution.py:80
  75.7 0.8 copy.79
  76.6 0.0 copy-start.10
  76.6 18.1 %reduce-window.6 = s32[64,16,128]{2,1,0:T(8,128)S(1)} reduce-window(s32[64,16,128]{2,1,0:T(8,128)S(1)} %fusion.17, s32[]{:T(128)} %constant.50.clone.1), window={size=1x1x128 pad=0_0x0_0x127_0}, to_apply=%region_1.2 | reduce-window | flops 16646144 | bytes 1048580 | tf_op jit(solution)/shard_map/reduce-window
  94.7 0.2 slice.20
  94.9 0.4 copy.107
  95.4 0.2 reduce-window.9
  95.6 0.2 broadcast_add_fusion
  95.8 0.3 fusion.12
  96.1 0.0 copy-start.13
  96.1 0.0 copy-start.11
  96.1 1.0 reshape.198
  97.1 0.2 reshape.177
  97.3 0.0 copy-start.2
  97.4 6.6 %scatter_custom_fusion = bf16[4096,128]{1,0:T(8,128)(2,1)S(1)} fusion(s32[2048]{0:T(1024)S(1)} %bitcast.70, bf16[2048,128]{1,0:T(8,128)(2,1)} %reshape.198, bf16[]{:T(256)} %constant.57.clone.1), kind=kCustom, calls=%fused_computation.32 | custom fusion | bytes 1049088 | tf_op jit(solution)/shard_map/scatter | solution.py:50
  104.0 0.0 copy-start.7
  104.0 0.5 fusion.20
  104.5 0.3 fusion
  104.8 0.1 copy-done.3
  104.9 0.2 copy-done.7
  105.1 2.3 add_divide_fusion
  107.4 7.6 %gather_fusion = f32[2048,128]{1,0:T(8,128)} fusion(f32[4096,128]{1,0:T(8,128)S(1)} %bitcast.51, s32[2048]{0:T(1024)S(1)} %broadcast_clamp_fusion), kind=kCustom, calls=%fused_computation | custom fusion | bytes 2105344 | tf_op jit(solution)/shard_map/gather | solution.py:86
  115.0 1.6 multiply_reduce_fusion.1
  116.5 0.1 reduce_sum.55
  116.6 0.9 broadcast_multiply_fusion
  117.6 0.7 mul.105
  118.2 7.4 %scatter_custom_fusion.1 = bf16[4096,128]{1,0:T(8,128)(2,1)S(1)} fusion(s32[2048]{0:T(1024)} %bitcast.71, f32[2048,128]{1,0:T(8,128)} %copy-done.2, f32[2048]{0:T(1024)} %mul.105, bf16[]{:T(256)} %constant.57.clone.1), kind=kCustom, calls=%fused_computation.23 | custom fusion | flops 524288 | bytes 2105856 | tf_op jit(solution)/shard_map/scatter | solution.py:93
  125.7 0.6 multiply_reduce_fusion
  126.3 0.0 copy-start.8
  126.3 0.9 copy-done.1
  127.2 1.4 fusion.3
  128.7 0.6 multiply_convert_fusion
  129.3 0.6 copy-done.4
  129.9 0.5 convolution_multiply_fusion.2
  130.4 1.0 copy.92
  131.4 0.2 copy.93
  131.6 2.2 pad_maximum_fusion
  133.8 0.0 reduce-scatter.2.cloned.1.call-update
  133.9 0.0 all-reduce.2.cloned.1.call-start
  133.9 0.2 reshape.169
  134.1 0.3 mul.96
  134.4 1.2 fusion.6
  135.6 64.0 %reduce-scatter.2.cloned.1.call-done = f32[16,2048]{1,0:T(8,128)} async-done(((f32[128,2048]{1,0:T(8,128)}), f32[16,2048]{1,0:T(8,128)}) %reduce-scatter.2.cloned.1.call-update) | async-done | bytes 131088 | tf_op jit(solution)/shard_map/reduce_scatter | solution.py:140
  199.6 0.0 all-reduce.2.cloned.1.call-update
  199.6 0.0 copy-start.12
  199.6 0.4 convolution_multiply_fusion
  200.1 0.7 copy.94
  200.7 0.7 copy.87
  201.4 6.2 %gather_fusion.1 = bf16[2048,128]{1,0:T(8,128)(2,1)S(1)} fusion(bf16[4096,128]{1,0:T(8,128)(2,1)S(1)} %bitcast.52, s32[2048]{0:T(1024)S(1)} %copy-done.12), kind=kCustom, calls=%fused_computation.1 | custom fusion | bytes 1056768 | tf_op jit(solution)/shard_map/gather | solution.py:138
  207.6 1.0 convert_element_type.49
  208.6 24.1 %all-reduce.2.cloned.1.call-done = f32[16,2048]{1,0:T(8,128)} async-done(((f32[16,2048]{1,0:T(8,128)}), f32[16,2048]{1,0:T(8,128)}) %all-reduce.2.cloned.1.call-update) | async-done | bytes 131088 | tf_op jit(solution)/shard_map/psum | solution.py:141
  232.7 1.5 fusion.19
  (23 shorter events, 0.1 us)
Async XLA Ops:
  7.2 192.4 %reduce-scatter.2.cloned.1.call-start = ((), (), s32[]{:S(2)}) async-start(), calls=%async_computation.1 | async-start | bytes 1179648 | tf_op jit(solution)/shard_map/reduce_scatter | solution.py:140
  76.6 19.5 %copy-start.10 = (bf16[128,2048]{1,0:T(8,128)(2,1)S(1)}, bf16[128,2048]{1,0:T(8,128)(2,1)}, u32[]{:S(2)}) copy-start(bf16[128,2048]{1,0:T(8,128)(2,1)} %param.7) | copy-start | bytes 1572868
  94.7 2.4 %copy-start.9 = (bf16[128,2048]{1,0:T(8,128)(2,1)S(1)}, bf16[128,2048]{1,0:T(8,128)(2,1)}, u32[]{:S(2)}) copy-start(bf16[128,2048]{1,0:T(8,128)(2,1)} %param.12) | copy-start | bytes 1572868
  96.1 7.9 %copy-start.13 = (s32[2048,1]{0,1:T(1,128)}, s32[2048,1]{0,1:T(1,128)S(1)}, u32[]{:S(2)}) copy-start(s32[2048,1]{0,1:T(1,128)S(1)} %compare_select_fusion) | copy-start | bytes 24580
  96.1 11.3 %copy-start.11 = (s32[2048]{0:T(1024)}, s32[2048]{0:T(1024)S(1)}, u32[]{:S(2)}) copy-start(s32[2048]{0:T(1024)S(1)} %broadcast_clamp_fusion) | copy-start | bytes 24580
  97.3 17.6 %copy-start.2 = (f32[2048,128]{1,0:T(8,128)}, f32[2048,128]{1,0:T(8,128)S(1)}, u32[]{:S(2)}) copy-start(f32[2048,128]{1,0:T(8,128)S(1)} %reshape.177) | copy-start | bytes 3145732
  103.9 1.0 copy-start.3
  104.0 1.2 copy-start.7
  104.5 2.9 %copy-start = (f32[8,512,128]{1,2,0:T(8,128)}, f32[8,512,128]{1,2,0:T(8,128)S(1)}, u32[]{:S(2)}) copy-start(f32[8,512,128]{1,2,0:T(8,128)S(1)} %get-tuple-element.28) | copy-start | bytes 6291460
  125.6 1.6 copy-start.1
  126.3 2.4 copy-start.8
  128.7 1.2 copy-start.4
  129.9 1.5 copy-start.6
  131.4 2.5 %copy-start.5 = (f32[2048,128]{1,0:T(8,128)S(1)}, f32[2048,128]{1,0:T(8,128)}, u32[]{:S(2)}) copy-start(f32[2048,128]{1,0:T(8,128)} %gather_fusion) | copy-start | bytes 3145732
  133.9 98.9 %all-reduce.2.cloned.1.call-start = ((), (), s32[]{:S(2)}) async-start(), calls=%async_computation.2 | async-start | bytes 262144 | tf_op jit(solution)/shard_map/psum | solution.py:141
  199.6 1.8 copy-start.12
Sparse Core Ops, SparseCore 0:
  134.0 65.5 reduce-scatter.1
  201.9 30.7 all-reduce.1
where the time goes:
time: 242 us; the launch traced here: 241 us
  waiting for transfers between devices  88.2 us (36%)
  blocking collectives  63.7 us (26%)
  other arithmetic  35.1 us (15%)
  local copies, waits for them, and re-layouts  34 us (14%)
  between operations  14.4 us (6%)
  matrix products  5.69 us (2%)
    reduce_scatter x1, waiting for transfers between devices, local(): share = lax.psum_scatter(grads, 'ctx', scatter_dimension=0, tiled=True)  64 us
    all_gather x1, blocking collectives, local(): lax.all_gather(prefix_keys, 'ctx', axis=0, tiled=True)  32.8 us
    all_gather x1, blocking collectives, local(): lax.all_gather(prefix_values, 'ctx', axis=0, tiled=True)  31 us
    psum x1, waiting for transfers between devices, local(): summed = lax.psum(share, 'sample')  24.1 us
    another operation x3, other arithmetic  18.5 us
    gather x1, local copies, waits for them, and re-layouts, local(): output.reshape(EXPERTS * CAP, HEAD)[slots].reshape(rows, TOPK, HEAD)  7.56 us
    scatter x1, other arithmetic, local(): jnp.zeros((EXPERTS * CAP, HEAD), jnp.bfloat16).at[slots]  7.39 us
    scatter x1, local copies, waits for them, and re-layouts, local(): jnp.zeros((EXPERTS * CAP, HEAD), jnp.bfloat16).at[slots]  6.57 us
  transfers between devices with their start and end apart: 2, of which 2 were waited for; matrix products, arithmetic and copies ran while one was open for 4% of the time, Pallas kernels for 0%

commit v1 on v0

v1 whole, which is shorter than its diff:
```python
import functools
import jax
import jax.numpy as jnp
from jax import lax
from jax.experimental import pallas as pl
from jax.experimental.pallas import tpu as pltpu
from jax.sharding import PartitionSpec as P

HEAD = 128
EXPERTS = 64
CLEN = 1024
SCALE = HEAD ** (-0.5)
LOG2E = 1.4426950408889634
F32 = jnp.float32
BF16 = jnp.bfloat16
AXES = ("sample", "ctx")
PICKS = 2


def grads_kernel(per_head, halves, info, q_ref, do_ref, ex_ref, gate_ref, *refs):
    blocks, (mine_ref, theirs_ref, prob_ref, ds_ref, gg_ref), scratch = refs[: 2 * halves], refs[2 * halves : 2 * halves + 5], refs[2 * halves + 5 :]
    kp, vp, q4, do4, p2, ds2 = scratch
    tokens, topk = ex_ref.shape
    own = blocks[0].shape[0] // 2
    total = 2 * halves * own
    pairs = kp.shape[1] // HEAD
    for b, ref in enumerate(blocks):
        for h in range(2 * pairs):
            rows = pl.ds((h % 2) * total + b * own, own)
            cols = pl.ds((h // 2) * HEAD, HEAD)
            kp[rows, cols] = ref[:own, h * HEAD : (h + 1) * HEAD]
            vp[rows, cols] = ref[own:, h * HEAD : (h + 1) * HEAD]
    head = ex_ref[...] // per_head
    pair = head // 2
    head_t = jnp.transpose(head.astype(F32))
    odd_t = head_t - 2.0 * jnp.floor(head_t * 0.5)
    live = (lax.broadcasted_iota(jnp.int32, (topk, tokens), 1) < info[0]).astype(F32)
    factor = jnp.transpose(gate_ref[...]) * live
    gates = []
    for c in range(topk // PICKS):
        lo, hi = c * PICKS * tokens, (c + 1) * PICKS * tokens
        odd, fac = [], []
        for k in range(c * PICKS, (c + 1) * PICKS):
            rows = pl.ds(k * tokens, tokens)
            q = q_ref[:, k * HEAD : (k + 1) * HEAD]
            do = do_ref[:, k * HEAD : (k + 1) * HEAD]
            spread = jnp.broadcast_to(pair[:, k : k + 1], (tokens, HEAD))
            for j in range(pairs):
                hot = jnp.where(spread == j, 1.0, 0.0).astype(BF16)
                q4[rows, j * HEAD : (j + 1) * HEAD] = q * hot
                do4[rows, j * HEAD : (j + 1) * HEAD] = do * hot
            odd.append(odd_t[k : k + 1, :])
            fac.append(factor[k : k + 1, :])
        odd = jnp.concatenate(odd, axis=1)
        fac = jnp.concatenate(fac, axis=1)
        is_odd = odd > 0.5
        nt = (((1,), (1,)), ((), ()))
        s2 = lax.dot_general(kp[...], q4[lo:hi, :], nt, preferred_element_type=F32)
        s = jnp.where(is_odd, s2[total:], s2[:total])
        d2 = lax.dot_general(vp[...], do4[lo:hi, :], nt, preferred_element_type=F32)
        dp = jnp.where(is_odd, d2[total:], d2[:total])
        high = jnp.max(s, axis=0, keepdims=True)
        e = jnp.exp2((s - high) * (SCALE * LOG2E))
        prob = e * (1.0 / jnp.sum(e, axis=0, keepdims=True))
        delta = jnp.sum(prob * dp, axis=0, keepdims=True)
        gates.append(delta)
        pf = prob * fac
        ds = pf * (dp - delta)
        prob_ref[:, lo:hi] = pf.astype(BF16)
        ds_ref[:, lo:hi] = ds.astype(BF16)
        p2[:total, lo:hi] = jnp.where(is_odd, 0.0, pf).astype(BF16)
        p2[total:, lo:hi] = jnp.where(is_odd, pf, 0.0).astype(BF16)
        ds2[:total, lo:hi] = jnp.where(is_odd, 0.0, ds).astype(BF16)
        ds2[total:, lo:hi] = jnp.where(is_odd, ds, 0.0).astype(BF16)
    gg = jnp.concatenate([g[:, i * tokens : (i + 1) * tokens] for g in gates for i in range(PICKS)], axis=0)
    gg_ref[...] = jnp.transpose(gg * live)
    for offset, (left, right, times) in enumerate(((ds2, q4, SCALE), (p2, do4, 1.0))):
        out = jnp.dot(left[...], right[...], preferred_element_type=F32) * times
        for b in range(2 * halves):
            ref = mine_ref if b < halves else theirs_ref
            rows = pl.ds((b % halves) * 2 * own + offset * own, own)
            for h in range(2 * pairs):
                piece = out[(h % 2) * total + b * own : (h % 2) * total + (b + 1) * own, (h // 2) * HEAD : (h // 2 + 1) * HEAD]
                ref[rows, h * HEAD : (h + 1) * HEAD] = piece.astype(ref.dtype)


def rows_kernel(per_head, halves, ex_ref, prob_ref, ds_ref, *refs):
    blocks, (att_ref, dq_ref), (kt, vt) = refs[: 2 * halves], refs[2 * halves : 2 * halves + 2], refs[2 * halves + 2 :]
    tokens, topk = ex_ref.shape
    own = blocks[0].shape[0] // 2
    total = 2 * halves * own
    pairs = kt.shape[1] // total
    for h in range(2 * pairs):
        cols = slice(h * HEAD, (h + 1) * HEAD)
        for dst, part in ((kt, slice(0, own)), (vt, slice(own, 2 * own))):
            whole = jnp.concatenate([ref[part, cols] for ref in blocks], axis=0)
            dst[(h % 2) * HEAD : (h % 2 + 1) * HEAD, (h // 2) * total : (h // 2 + 1) * total] = jnp.transpose(whole)
    head_t = jnp.transpose((ex_ref[...] // per_head).astype(F32))
    pair_t = jnp.floor(head_t * 0.5)
    odd_t = head_t - 2.0 * pair_t
    for c in range(topk // PICKS):
        lo, hi = c * PICKS * tokens, (c + 1) * PICKS * tokens
        ks = range(c * PICKS, (c + 1) * PICKS)
        pair = jnp.concatenate([pair_t[k : k + 1, :] for k in ks], axis=1)
        is_odd = jnp.concatenate([odd_t[k : k + 1, :] for k in ks], axis=1) > 0.5
        hots = [jnp.broadcast_to(jnp.where(pair == j, 1.0, 0.0), (16, hi - lo)).astype(BF16) for j in range(pairs)]
        for src, left, out_ref, times in ((prob_ref, vt, att_ref, None), (ds_ref, kt, dq_ref, SCALE)):
            val = src[:, lo:hi].reshape(total // 16, 16, hi - lo)
            wide = jnp.concatenate([(val * hot[None]).reshape(total, hi - lo) for hot in hots], axis=0)
            out2 = jnp.dot(left[...], wide, preferred_element_type=F32)
            out = jnp.where(is_odd, out2[HEAD:], out2[:HEAD])
            if times is not None:
                out = out * times
            out = out.astype(BF16)
            for i, k in enumerate(ks):
                out_ref[:, k * HEAD : (k + 1) * HEAD] = jnp.transpose(out[:, i * tokens : (i + 1) * tokens])


def gather_pairs(n_sample, n_ctx, first, second):
    out = []
    for s in range(n_sample):
        for j in range(n_ctx):
            o = second if s % 2 else first
            src = j ^ o if n_ctx & (n_ctx - 1) == 0 else (j + o) % n_ctx
            out.append((s * n_ctx + src, s * n_ctx + j))
    return out


def swap_pairs(n_sample, n_ctx, bit):
    return [(s * n_ctx + j, (s ^ bit) * n_ctx + j) for s in range(n_sample) for j in range(n_ctx)]


def local(queries, experts, gate, prefix_keys, prefix_values, d_out, lengths):
    n_sample, n_ctx = lax.axis_size("sample"), lax.axis_size("ctx")
    tokens, topk = experts.shape
    own, width = prefix_keys.shape
    heads = width // HEAD
    per_head = EXPERTS // heads
    total = own * n_ctx
    halves = n_ctx // 2
    picked = tokens * topk
    pairs = heads // 2
    assert n_ctx % 2 == 0 and n_sample & (n_sample - 1) == 0 and n_sample > 1 and CLEN % tokens == 0

    begin = (lax.axis_index("sample") * n_ctx + lax.axis_index("ctx")) * tokens
    count = lax.dynamic_index_in_dim(lengths, begin // CLEN, 0, keepdims=True) - begin % CLEN

    offsets = list(range(1, n_ctx)) + [0]
    firsts, seconds = offsets[0::2], offsets[1::2]
    routes = [gather_pairs(n_sample, n_ctx, a, b) for a, b in zip(firsts, seconds, strict=True)]
    swap = swap_pairs(n_sample, n_ctx, 1)
    block = jnp.concatenate([prefix_keys, prefix_values], axis=0)
    got = [lax.ppermute(block, AXES, r) for r in routes]
    other = [lax.ppermute(g, AXES, swap) for g in got]
    blocks = got + other

    vmem = pl.BlockSpec(memory_space=pltpu.VMEM)
    smem = pl.BlockSpec(memory_space=pltpu.SMEM)
    flops = 2 * 4 * picked * total * width
    mine, theirs, prob, ds, gate_grad = pl.pallas_call(
        functools.partial(grads_kernel, per_head, halves),
        out_shape=(
            jax.ShapeDtypeStruct((halves * 2 * own, width), F32),
            jax.ShapeDtypeStruct((halves * 2 * own, width), BF16),
            jax.ShapeDtypeStruct((total, picked), BF16),
            jax.ShapeDtypeStruct((total, picked), BF16),
            jax.ShapeDtypeStruct((tokens, topk), F32),
        ),
        in_specs=[smem] + [vmem] * (4 + 2 * halves),
        out_specs=[vmem] * 5,
        scratch_shapes=[
            pltpu.VMEM((2 * total, pairs * HEAD), BF16),
            pltpu.VMEM((2 * total, pairs * HEAD), BF16),
            pltpu.VMEM((picked, pairs * HEAD), BF16),
            pltpu.VMEM((picked, pairs * HEAD), BF16),
            pltpu.VMEM((2 * total, picked), BF16),
            pltpu.VMEM((2 * total, picked), BF16),
        ],
        cost_estimate=pl.CostEstimate(flops=flops, bytes_accessed=4 << 20, transcendentals=picked * total),
        name="grads",
    )(count, queries, d_out, experts, gate, *blocks)

    attended, query_grad = pl.pallas_call(
        functools.partial(rows_kernel, per_head, halves),
        out_shape=(
            jax.ShapeDtypeStruct(queries.shape, BF16),
            jax.ShapeDtypeStruct(queries.shape, BF16),
        ),
        in_specs=[vmem] * (3 + 2 * halves),
        out_specs=[vmem] * 2,
        scratch_shapes=[
            pltpu.VMEM((2 * HEAD, pairs * total), BF16),
            pltpu.VMEM((2 * HEAD, pairs * total), BF16),
        ],
        cost_estimate=pl.CostEstimate(flops=flops // 2, bytes_accessed=2 << 20, transcendentals=0),
        name="rows",
    )(experts, prob, ds, *blocks)

    from_other = lax.ppermute(theirs, AXES, swap).astype(F32)
    parts = []
    for m, route in enumerate(routes):
        rows = slice(m * 2 * own, (m + 1) * 2 * own)
        back = [(dst, src) for src, dst in route]
        parts.append(lax.ppermute((mine[rows] + from_other[rows]).astype(BF16), AXES, back))
    share = sum(p.astype(F32) for p in parts)
    share = share + lax.ppermute(share, AXES, swap)
    bit = 2
    while bit < n_sample:
        share = share + lax.ppermute(share, AXES, swap_pairs(n_sample, n_ctx, bit))
        bit *= 2
    return (attended, query_grad, gate_grad, share[:own], share[own:])


def solution(mesh):
    row = P(("sample", "ctx"), None)
    return jax.shard_map(
        local,
        mesh=mesh,
        in_specs=(row, row, row, P("ctx", None), P("ctx", None), row, P()),
        out_specs=(row, row, row, P("ctx", None), P("ctx", None)),
        check_vma=False,
    )
```

time: 242 us -> 51.6 us (0.21)
  waiting for transfers between devices: 88.2 us -> 11.8 us
  blocking collectives: 63.7 us -> 0 us
  other arithmetic: 35.1 us -> 0.16 us
  local copies, waits for them, and re-layouts: 34 us -> 6.77 us
  starting transfers between devices: 0.08 us -> 21.5 us
  between operations: 14.4 us -> 1.5 us
  Pallas kernels: 0 us -> 9.46 us
  matrix products: 5.69 us -> 0 us
    reduce_scatter x1 -> x0, waiting for transfers between devices: 64 us -> none  [local(): share = lax.psum_scatter(grads, 'ctx', scatter_dimension=0, tiled=True)]
    all_gather x2 -> x0, blocking collectives: 63.7 us -> none  [the longest x1 32.8 us: local(): lax.all_gather(prefix_keys, 'ctx', axis=0, tiled=True)]
    psum x1 -> x0, waiting for transfers between devices: 24.1 us -> none  [local(): summed = lax.psum(share, 'sample')]
    ppermute x0 -> x15, starting transfers between devices: none -> 21.5 us  [the longest x4 10 us: local(): got = [lax.ppermute(block, AXES, r) for r in routes]]
    another operation x4 -> x0, other arithmetic: 18.5 us -> none
    gather x2 -> x0, local copies, waits for them, and re-layouts: 13.7 us -> none  [the longest x1 7.56 us: local(): output.reshape(EXPERTS * CAP, HEAD)[slots].reshape(rows, TOPK, HEAD)]
    ppermute x0 -> x15, waiting for transfers between devices: none -> 11.8 us  [the longest x4 6.32 us: local(): got = [lax.ppermute(block, AXES, r) for r in routes]]
    pallas_call x0 -> x2, Pallas kernels: none -> 9.46 us  [the longest x1 5.73 us: local(): pl.pallas_call(functools.partial(grads_kernel, per_head, halves), out_sha...]
  transfers between devices with their start and end apart: 2 -> 15, of which waited for: 2 -> 6; matrix products, arithmetic and copies ran while one was open for 4% -> 5% of each run, Pallas kernels for 0% -> 7%
where the time goes in v1:
time: 51.6 us; the launch traced here: 51.2 us
  starting transfers between devices  21.5 us (42%)
  waiting for transfers between devices  11.8 us (23%)
  Pallas kernels  9.46 us (18%)
  local copies, waits for them, and re-layouts  6.77 us (13%)
  between operations  1.5 us (3%)
    ppermute x4, starting transfers between devices, local(): got = [lax.ppermute(block, AXES, r) for r in routes]  10 us
    ppermute x4, starting transfers between devices, local(): lax.ppermute((mine[rows] + from_other[rows]).astype(BF16), AXES, back)  8.77 us
    ppermute x4, waiting for transfers between devices, local(): got = [lax.ppermute(block, AXES, r) for r in routes]  6.32 us
    pallas_call x1, Pallas kernels, local(): pl.pallas_call(functools.partial(grads_kernel, per_head, halves), out_sha...  5.73 us
    unnamed x32, local copies, waits for them, and re-layouts  5.53 us
    pallas_call x1, Pallas kernels, local(): pl.pallas_call(functools.partial(rows_kernel, per_head, halves), out_shap...  3.74 us
    ppermute x4, waiting for transfers between devices, local(): lax.ppermute((mine[rows] + from_other[rows]).astype(BF16), AXES, back)  2.75 us
    ppermute x1, starting transfers between devices, local(): share = share + lax.ppermute(share, AXES, swap_pairs(n_sample, n_ctx, bit))  1.56 us
  transfers between devices with their start and end apart: 15, of which 6 were waited for; matrix products, arithmetic and copies ran while one was open for 5% of the time, Pallas kernels for 7%

profile of v1, /device:TPU:0, one launch (start us, length us, event | category | flops | bytes accessed | tf_op | source)
XLA Modules:
  0.0 51.2 jit_solution(2499626138815917053)
XLA Ops:
  0.6 0.0 copy-start.2
  0.6 0.8 %constant_dynamic-update-slice_fusion.1 = bf16[32,1024]{1,0:T(8,128)(2,1)S(1)} fusion(bf16[16,1024]{1,0:T(8,128)(2,1)} %param.10), kind=kLoop, calls=%fused_computation.10 | loop fusion | bytes 65536
  1.4 0.0 copy-done.2
  1.4 3.1 %collective-permute-start = (bf16[32,1024]{1,0:T(8,128)(2,1)S(1)}, bf16[32,1024]{1,0:T(8,128)(2,1)S(1)}, u32[]{:S(2)}, u32[]{:S(2)}) collective-permute-start(bf16[32,1024]{1,0:T(8,128)(2,1)S(1)} %constant_dynamic-update-slice_fusion), channel_id=1, source_target_pairs={{1,0},{0,1},{3,2},{2,3},{5,4},{4,5},{7,6},{6,7},{10,8},{11,9},{8,1... | collective-permute-start | bytes 196616 | tf_op jit(solution)/shard_map/ppermute | solution.py:153
  4.5 1.5 %collective-permute-start.1 = (bf16[32,1024]{1,0:T(8,128)(2,1)S(1)}, bf16[32,1024]{1,0:T(8,128)(2,1)S(1)}, u32[]{:S(2)}, u32[]{:S(2)}) collective-permute-start(bf16[32,1024]{1,0:T(8,128)(2,1)S(1)} %constant_dynamic-update-slice_fusion), channel_id=1, source_target_pairs={{3,0},{2,1},{1,2},{0,3},{7,4},{6,5},{5,6},{4,7},{12,8},{13,9},{14,... | collective-permute-start | bytes 196616 | tf_op jit(solution)/shard_map/ppermute | solution.py:153
  6.0 3.5 %collective-permute-start.2 = (bf16[32,1024]{1,0:T(8,128)(2,1)S(1)}, bf16[32,1024]{1,0:T(8,128)(2,1)S(1)}, u32[]{:S(2)}, u32[]{:S(2)}) collective-permute-start(bf16[32,1024]{1,0:T(8,128)(2,1)S(1)} %constant_dynamic-update-slice_fusion), channel_id=1, source_target_pairs={{5,0},{4,1},{7,2},{6,3},{1,4},{0,5},{3,6},{2,7},{14,8},{15,9},{12,... | collective-permute-start | bytes 196616 | tf_op jit(solution)/shard_map/ppermute | solution.py:153
  9.5 1.9 %collective-permute-start.3 = (bf16[32,1024]{1,0:T(8,128)(2,1)S(1)}, bf16[32,1024]{1,0:T(8,128)(2,1)S(1)}, u32[]{:S(2)}, u32[]{:S(2)}) collective-permute-start(bf16[32,1024]{1,0:T(8,128)(2,1)S(1)} %constant_dynamic-update-slice_fusion), channel_id=1, source_target_pairs={{7,0},{6,1},{5,2},{4,3},{3,4},{2,5},{1,6},{0,7},{8,8},{9,9},{10,10... | collective-permute-start | bytes 196616 | tf_op jit(solution)/shard_map/ppermute | solution.py:153
  11.5 0.0 collective-permute-done.refs_0_
  11.5 0.0 copy-start.5
  11.5 0.1 collective-permute-start.4
  11.6 0.0 collective-permute-done.1.refs_1_
  11.6 0.0 copy-start.6
  11.6 0.5 collective-permute-start.5
  12.1 1.4 %collective-permute-done.2.refs_2_ = bf16[32,1024]{1,0:T(8,128)(2,1)S(1)} collective-permute-done((bf16[32,1024]{1,0:T(8,128)(2,1)S(1)}, bf16[32,1024]{1,0:T(8,128)(2,1)S(1)}, u32[]{:S(2)}, u32[]{:S(2)}) %collective-permute-start.2) | collective-permute-done | bytes 65568 | tf_op jit(solution)/shard_map/ppermute | solution.py:153
  13.5 0.0 copy-start.7
  13.5 0.0 collective-permute-start.6
  13.5 4.9 %collective-permute-done.3.refs_3_ = bf16[32,1024]{1,0:T(8,128)(2,1)S(1)} collective-permute-done((bf16[32,1024]{1,0:T(8,128)(2,1)S(1)}, bf16[32,1024]{1,0:T(8,128)(2,1)S(1)}, u32[]{:S(2)}, u32[]{:S(2)}) %collective-permute-start.3) | collective-permute-done | bytes 65568 | tf_op jit(solution)/shard_map/ppermute | solution.py:153
  18.4 0.0 copy-start.8
  18.4 0.0 collective-permute-start.7
  18.4 0.0 copy-start.3
  18.4 0.7 %copy-done.3 = s32[128,16]{0,1:T(8,128)S(1)} copy-done((s32[128,16]{0,1:T(8,128)S(1)}, s32[128,16]{0,1:T(8,128)}, u32[]{:S(2)}) %copy-start.3) | copy-done | bytes 8216
  19.1 0.0 copy-start.4
  19.1 0.7 %copy.14.ex_ref = s32[128,16]{1,0:T(8,128)} copy(s32[128,16]{0,1:T(8,128)S(1)} %copy-done.3) | data formatting | bytes 16384 | tf_op args[1]
  19.8 0.0 copy-done.4
  19.8 0.7 %copy.13.gate_ref = f32[128,16]{1,0:T(8,128)} copy(f32[128,16]{0,1:T(8,128)S(1)} %copy-done.4) | data formatting | bytes 16384 | tf_op args[2]
  20.6 0.0 copy-done.5
  20.6 0.0 copy-done.6
  20.6 0.0 copy-done.7
  20.6 0.6 %copy-done.13 = s32[4]{0:T(128)S(1)} copy-done((s32[4]{0:T(128)S(1)}, s32[4]{0:T(128)}, u32[]{:S(2)}) %copy-start.13) | copy-done | bytes 40
  21.2 0.6 %dynamic_slice.4 = s32[1]{0:T(128)} dynamic-slice(s32[4]{0:T(128)S(1)} %copy-done.13, s32[]{:T(128)S(6)} %select_n.16), dynamic_slice_sizes={1} | dynamic-slice | bytes 12 | tf_op jit(solution)/shard_map/jit(dynamic_index_in_dim)/dynamic_slice | solution.py:146
  22.5 0.0 collective-permute-done.4.refs_4_
  22.5 0.0 copy-start.9
  22.5 0.0 collective-permute-done.5.refs_5_
  22.5 0.0 copy-start.10
  22.5 0.0 collective-permute-done.6.refs_6_
  22.5 0.0 copy-start.11
  22.5 0.0 collective-permute-done.7.refs_7_
  22.6 0.0 copy-done.8
  22.6 0.5 %copy-done.9 = bf16[32,1024]{1,0:T(8,128)(2,1)} copy-done((bf16[32,1024]{1,0:T(8,128)(2,1)}, bf16[32,1024]{1,0:T(8,128)(2,1)S(1)}, u32[]{:S(2)}) %copy-start.9) | copy-done | bytes 65560
  23.1 0.0 copy-done.10
  23.1 0.0 copy-done.11
  23.2 0.6 %copy-done.12 = bf16[32,1024]{1,0:T(8,128)(2,1)} copy-done((bf16[32,1024]{1,0:T(8,128)(2,1)}, bf16[32,1024]{1,0:T(8,128)(2,1)S(1)}, u32[]{:S(2)}) %copy-start.12) | copy-done | bytes 65560
  23.8 5.7 %grads.1 = (f32[128,1024]{1,0:T(8,128)}, bf16[128,1024]{1,0:T(8,128)(2,1)}, bf16[128,2048]{1,0:T(8,128)(2,1)}, bf16[128,2048]{1,0:T(8,128)(2,1)}, f32[128,16]{1,0:T(8,128)}) custom-call(s32[1]{0:T(128)S(6)} %sub.12.info, bf16[128,2048]{1,0:T(8,128)(2,1)} %q_ref.1, bf16[128,2048]{1,0:T(8,128)(2,1)} %do_ref.1, s32[128,16]{1,0:T(8,128)} %copy.14.ex_ref, ...), custom_call_target="tpu_custom_call" | custom-call | flops 2147483648 | bytes 4194304 | tf_op jit(solution)/shard_map/grads/pallas_call | solution.py:160
  29.5 0.5 %collective-permute-start.8 = (bf16[128,1024]{1,0:T(8,128)(2,1)}, bf16[128,1024]{1,0:T(8,128)(2,1)S(1)}, u32[]{:S(2)}, u32[]{:S(2)}) collective-permute-start(bf16[128,1024]{1,0:T(8,128)(2,1)} %get-tuple-element.18), channel_id=1, source_target_pairs={{0,8},{1,9},{2,10},{3,11},{4,12},{5,13},{6,14},{7,15},{8,0},{9,1},... | collective-permute-start | bytes 786440 | tf_op jit(solution)/shard_map/ppermute | solution.py:199
  30.1 1.4 %collective-permute-done.8 = bf16[128,1024]{1,0:T(8,128)(2,1)S(1)} collective-permute-done((bf16[128,1024]{1,0:T(8,128)(2,1)}, bf16[128,1024]{1,0:T(8,128)(2,1)S(1)}, u32[]{:S(2)}, u32[]{:S(2)}) %collective-permute-start.8) | collective-permute-done | bytes 262176 | tf_op jit(solution)/shard_map/ppermute | solution.py:199
  31.5 0.0 copy-done
  31.5 0.1 fusion.3
  31.6 0.1 collective-permute-start.10
  31.6 1.7 %collective-permute-start.11 = (bf16[32,1024]{1,0:T(8,128)(2,1)S(1)}, bf16[32,1024]{1,0:T(8,128)(2,1)S(1)}, u32[]{:S(2)}, u32[]{:S(2)}) collective-permute-start(bf16[32,1024]{1,0:T(8,128)(2,1)S(1)} %get-tuple-element.26), channel_id=1, source_target_pairs={{0,5},{1,4},{2,7},{3,6},{4,1},{5,0},{6,3},{7,2},{8,14},{9,15},{10,... | collective-permute-start | bytes 196616 | tf_op jit(solution)/shard_map/ppermute | solution.py:204
  33.3 5.4 %collective-permute-start.12 = (bf16[32,1024]{1,0:T(8,128)(2,1)S(1)}, bf16[32,1024]{1,0:T(8,128)(2,1)S(1)}, u32[]{:S(2)}, u32[]{:S(2)}) collective-permute-start(bf16[32,1024]{1,0:T(8,128)(2,1)S(1)} %get-tuple-element.25), channel_id=1, source_target_pairs={{0,7},{1,6},{2,5},{3,4},{4,3},{5,2},{6,1},{7,0},{8,8},{9,9},{10,10... | collective-permute-start | bytes 196616 | tf_op jit(solution)/shard_map/ppermute | solution.py:204
  38.8 1.6 %collective-permute-start.9 = (bf16[32,1024]{1,0:T(8,128)(2,1)S(1)}, bf16[32,1024]{1,0:T(8,128)(2,1)S(1)}, u32[]{:S(2)}, u32[]{:S(2)}) collective-permute-start(bf16[32,1024]{1,0:T(8,128)(2,1)S(1)} %get-tuple-element.24), channel_id=1, source_target_pairs={{0,1},{1,0},{2,3},{3,2},{4,5},{5,4},{6,7},{7,6},{8,10},{9,11},{10,... | collective-permute-start | bytes 196616 | tf_op jit(solution)/shard_map/ppermute | solution.py:204
  40.4 0.0 collective-permute-done.10
  40.4 0.0 collective-permute-done.11
  40.4 1.8 %collective-permute-done.12 = bf16[32,1024]{1,0:T(8,128)(2,1)S(1)} collective-permute-done((bf16[32,1024]{1,0:T(8,128)(2,1)S(1)}, bf16[32,1024]{1,0:T(8,128)(2,1)S(1)}, u32[]{:S(2)}, u32[]{:S(2)}) %collective-permute-start.12) | collective-permute-done | bytes 65568 | tf_op jit(solution)/shard_map/ppermute | solution.py:204
  42.2 0.9 %collective-permute-done.9 = bf16[32,1024]{1,0:T(8,128)(2,1)S(1)} collective-permute-done((bf16[32,1024]{1,0:T(8,128)(2,1)S(1)}, bf16[32,1024]{1,0:T(8,128)(2,1)S(1)}, u32[]{:S(2)}, u32[]{:S(2)}) %collective-permute-start.9) | collective-permute-done | bytes 65568 | tf_op jit(solution)/shard_map/ppermute | solution.py:204
  43.1 0.0 copy-start.1
  43.1 0.1 collective-permute-start.13
  43.2 1.3 %collective-permute-done.13 = f32[32,1024]{1,0:T(8,128)S(1)} collective-permute-done((f32[32,1024]{1,0:T(8,128)S(1)}, f32[32,1024]{1,0:T(8,128)S(1)}, u32[]{:S(2)}, u32[]{:S(2)}) %collective-permute-start.13) | collective-permute-done | bytes 131104 | tf_op jit(solution)/shard_map/ppermute | solution.py:206
  44.6 1.6 %collective-permute-start.14 = (f32[32,1024]{1,0:T(8,128)S(1)}, f32[32,1024]{1,0:T(8,128)S(1)}, u32[]{:S(2)}, u32[]{:S(2)}) collective-permute-start(f32[32,1024]{1,0:T(8,128)S(1)} %add.49), channel_id=1, source_target_pairs={{0,16},{1,17},{2,18},{3,19},{4,20},{5,21},{6,22},{7,23},{8,24},{9,... | collective-permute-start | bytes 393224 | tf_op jit(solution)/shard_map/ppermute | solution.py:209
  46.1 0.0 copy-done.1
  46.1 0.7 %copy.15 = f32[128,16]{0,1:T(8,128)} copy(f32[128,16]{1,0:T(8,128)S(1)} %copy-done.1) | data formatting | bytes 16384
  46.8 3.7 %rows.1 = (bf16[128,2048]{1,0:T(8,128)(2,1)}, bf16[128,2048]{1,0:T(8,128)(2,1)}) custom-call(s32[128,16]{1,0:T(8,128)} %copy.14.ex_ref, bf16[128,2048]{1,0:T(8,128)(2,1)} %get-tuple-element.12.prob_ref, bf16[128,2048]{1,0:T(8,128)(2,1)} %get-tuple-element.13.ds_ref, bf16[32,1024]{1,0:T(8,128)(2,1)} %copy-done.5, bf16[32,1024]{1,0:T(8,128)(2,1)} %copy-done.6, ...), custom_call_target="tpu_custom_call" | custom-call | flops 1073741824 | bytes 2097152 | tf_op jit(solution)/shard_map/rows/pallas_call | solution.py:183
  50.6 0.0 collective-permute-done.14
  50.6 0.7 %fusion.4 = (f32[16,1024]{1,0:T(8,128)}, f32[16,1024]{1,0:T(8,128)}) fusion(f32[32,1024]{1,0:T(8,128)S(1)} %add.50), kind=kLoop, calls=%fused_computation.11 | loop fusion | bytes 262144 | tf_op jit(solution)/shard_map/slice | solution.py:211
  (8 shorter events, 0.1 us)
Async XLA Ops:
  0.6 0.8 %copy-start.2 = (bf16[16,1024]{1,0:T(8,128)(2,1)S(1)}, bf16[16,1024]{1,0:T(8,128)(2,1)}, u32[]{:S(2)}) copy-start(bf16[16,1024]{1,0:T(8,128)(2,1)} %param.11) | copy-start | bytes 98308
  1.4 10.0 %collective-permute-start = (bf16[32,1024]{1,0:T(8,128)(2,1)S(1)}, bf16[32,1024]{1,0:T(8,128)(2,1)S(1)}, u32[]{:S(2)}, u32[]{:S(2)}) collective-permute-start(bf16[32,1024]{1,0:T(8,128)(2,1)S(1)} %constant_dynamic-update-slice_fusion), channel_id=1, source_target_pairs={{1,0},{0,1},{3,2},{2,3},{5,4},{4,5},{7,6},{6,7},{10,8},{11,9},{8,1... | collective-permute-start | bytes 196616 | tf_op jit(solution)/shard_map/ppermute | solution.py:153
  4.5 7.1 %collective-permute-start.1 = (bf16[32,1024]{1,0:T(8,128)(2,1)S(1)}, bf16[32,1024]{1,0:T(8,128)(2,1)S(1)}, u32[]{:S(2)}, u32[]{:S(2)}) collective-permute-start(bf16[32,1024]{1,0:T(8,128)(2,1)S(1)} %constant_dynamic-update-slice_fusion), channel_id=1, source_target_pairs={{3,0},{2,1},{1,2},{0,3},{7,4},{6,5},{5,6},{4,7},{12,8},{13,9},{14,... | collective-permute-start | bytes 196616 | tf_op jit(solution)/shard_map/ppermute | solution.py:153
  6.0 7.5 %collective-permute-start.2 = (bf16[32,1024]{1,0:T(8,128)(2,1)S(1)}, bf16[32,1024]{1,0:T(8,128)(2,1)S(1)}, u32[]{:S(2)}, u32[]{:S(2)}) collective-permute-start(bf16[32,1024]{1,0:T(8,128)(2,1)S(1)} %constant_dynamic-update-slice_fusion), channel_id=1, source_target_pairs={{5,0},{4,1},{7,2},{6,3},{1,4},{0,5},{3,6},{2,7},{14,8},{15,9},{12,... | collective-permute-start | bytes 196616 | tf_op jit(solution)/shard_map/ppermute | solution.py:153
  9.5 8.8 %collective-permute-start.3 = (bf16[32,1024]{1,0:T(8,128)(2,1)S(1)}, bf16[32,1024]{1,0:T(8,128)(2,1)S(1)}, u32[]{:S(2)}, u32[]{:S(2)}) collective-permute-start(bf16[32,1024]{1,0:T(8,128)(2,1)S(1)} %constant_dynamic-update-slice_fusion), channel_id=1, source_target_pairs={{7,0},{6,1},{5,2},{4,3},{3,4},{2,5},{1,6},{0,7},{8,8},{9,9},{10,10... | collective-permute-start | bytes 196616 | tf_op jit(solution)/shard_map/ppermute | solution.py:153
  11.5 9.1 %copy-start.5 = (bf16[32,1024]{1,0:T(8,128)(2,1)}, bf16[32,1024]{1,0:T(8,128)(2,1)S(1)}, u32[]{:S(2)}) copy-start(bf16[32,1024]{1,0:T(8,128)(2,1)S(1)} %collective-permute-done.refs_0_) | copy-start | bytes 196612
  11.5 11.0 %collective-permute-start.4 = (bf16[32,1024]{1,0:T(8,128)(2,1)S(1)}, bf16[32,1024]{1,0:T(8,128)(2,1)S(1)}, u32[]{:S(2)}, u32[]{:S(2)}) collective-permute-start(bf16[32,1024]{1,0:T(8,128)(2,1)S(1)} %collective-permute-done.refs_0_), channel_id=1, source_target_pairs={{0,8},{1,9},{2,10},{3,11},{4,12},{5,13},{6,14},{7,15},{8,0},{9,1},... | collective-permute-start | bytes 196616 | tf_op jit(solution)/shard_map/ppermute | solution.py:154
  11.6 9.0 %copy-start.6 = (bf16[32,1024]{1,0:T(8,128)(2,1)}, bf16[32,1024]{1,0:T(8,128)(2,1)S(1)}, u32[]{:S(2)}) copy-start(bf16[32,1024]{1,0:T(8,128)(2,1)S(1)} %collective-permute-done.1.refs_1_) | copy-start | bytes 196612
  11.6 10.9 %collective-permute-start.5 = (bf16[32,1024]{1,0:T(8,128)(2,1)S(1)}, bf16[32,1024]{1,0:T(8,128)(2,1)S(1)}, u32[]{:S(2)}, u32[]{:S(2)}) collective-permute-start(bf16[32,1024]{1,0:T(8,128)(2,1)S(1)} %collective-permute-done.1.refs_1_), channel_id=1, source_target_pairs={{0,8},{1,9},{2,10},{3,11},{4,12},{5,13},{6,14},{7,15},{8,0},{9,1},... | collective-permute-start | bytes 196616 | tf_op jit(solution)/shard_map/ppermute | solution.py:154
  13.5 7.1 %copy-start.7 = (bf16[32,1024]{1,0:T(8,128)(2,1)}, bf16[32,1024]{1,0:T(8,128)(2,1)S(1)}, u32[]{:S(2)}) copy-start(bf16[32,1024]{1,0:T(8,128)(2,1)S(1)} %collective-permute-done.2.refs_2_) | copy-start | bytes 196612
  13.5 9.1 %collective-permute-start.6 = (bf16[32,1024]{1,0:T(8,128)(2,1)S(1)}, bf16[32,1024]{1,0:T(8,128)(2,1)S(1)}, u32[]{:S(2)}, u32[]{:S(2)}) collective-permute-start(bf16[32,1024]{1,0:T(8,128)(2,1)S(1)} %collective-permute-done.2.refs_2_), channel_id=1, source_target_pairs={{0,8},{1,9},{2,10},{3,11},{4,12},{5,13},{6,14},{7,15},{8,0},{9,1},... | collective-permute-start | bytes 196616 | tf_op jit(solution)/shard_map/ppermute | solution.py:154
  18.4 4.2 %copy-start.8 = (bf16[32,1024]{1,0:T(8,128)(2,1)}, bf16[32,1024]{1,0:T(8,128)(2,1)S(1)}, u32[]{:S(2)}) copy-start(bf16[32,1024]{1,0:T(8,128)(2,1)S(1)} %collective-permute-done.3.refs_3_) | copy-start | bytes 196612
  18.4 4.2 %collective-permute-start.7 = (bf16[32,1024]{1,0:T(8,128)(2,1)S(1)}, bf16[32,1024]{1,0:T(8,128)(2,1)S(1)}, u32[]{:S(2)}, u32[]{:S(2)}) collective-permute-start(bf16[32,1024]{1,0:T(8,128)(2,1)S(1)} %collective-permute-done.3.refs_3_), channel_id=1, source_target_pairs={{0,8},{1,9},{2,10},{3,11},{4,12},{5,13},{6,14},{7,15},{8,0},{9,1},... | collective-permute-start | bytes 196616 | tf_op jit(solution)/shard_map/ppermute | solution.py:154
  18.4 0.7 %copy-start.3 = (s32[128,16]{0,1:T(8,128)S(1)}, s32[128,16]{0,1:T(8,128)}, u32[]{:S(2)}) copy-start(s32[128,16]{0,1:T(8,128)} %param.8) | copy-start | bytes 24580
  19.1 0.7 %copy-start.4 = (f32[128,16]{0,1:T(8,128)S(1)}, f32[128,16]{0,1:T(8,128)}, u32[]{:S(2)}) copy-start(f32[128,16]{0,1:T(8,128)} %param.9) | copy-start | bytes 24580
  20.6 0.7 %copy-start.13 = (s32[4]{0:T(128)S(1)}, s32[4]{0:T(128)}, u32[]{:S(2)}) copy-start(s32[4]{0:T(128)} %param.13) | copy-start | bytes 52
  22.5 0.6 %copy-start.9 = (bf16[32,1024]{1,0:T(8,128)(2,1)}, bf16[32,1024]{1,0:T(8,128)(2,1)S(1)}, u32[]{:S(2)}) copy-start(bf16[32,1024]{1,0:T(8,128)(2,1)S(1)} %collective-permute-done.4.refs_4_) | copy-start | bytes 196612
  22.5 0.6 %copy-start.10 = (bf16[32,1024]{1,0:T(8,128)(2,1)}, bf16[32,1024]{1,0:T(8,128)(2,1)S(1)}, u32[]{:S(2)}) copy-start(bf16[32,1024]{1,0:T(8,128)(2,1)S(1)} %collective-permute-done.5.refs_5_) | copy-start | bytes 196612
  22.5 0.6 %copy-start.11 = (bf16[32,1024]{1,0:T(8,128)(2,1)}, bf16[32,1024]{1,0:T(8,128)(2,1)S(1)}, u32[]{:S(2)}) copy-start(bf16[32,1024]{1,0:T(8,128)(2,1)S(1)} %collective-permute-done.6.refs_6_) | copy-start | bytes 196612
  23.2 0.6 %copy-start.12 = (bf16[32,1024]{1,0:T(8,128)(2,1)}, bf16[32,1024]{1,0:T(8,128)(2,1)S(1)}, u32[]{:S(2)}) copy-start(bf16[32,1024]{1,0:T(8,128)(2,1)S(1)} %collective-permute-done.7.refs_7_) | copy-start | bytes 196612
  29.5 2.0 %copy-start = (f32[128,1024]{1,0:T(8,128)S(1)}, f32[128,1024]{1,0:T(8,128)}, u32[]{:S(2)}) copy-start(f32[128,1024]{1,0:T(8,128)} %get-tuple-element.17) | copy-start | bytes 1572868
  29.5 1.9 %collective-permute-start.8 = (bf16[128,1024]{1,0:T(8,128)(2,1)}, bf16[128,1024]{1,0:T(8,128)(2,1)S(1)}, u32[]{:S(2)}, u32[]{:S(2)}) collective-permute-start(bf16[128,1024]{1,0:T(8,128)(2,1)} %get-tuple-element.18), channel_id=1, source_target_pairs={{0,8},{1,9},{2,10},{3,11},{4,12},{5,13},{6,14},{7,15},{8,0},{9,1},... | collective-permute-start | bytes 786440 | tf_op jit(solution)/shard_map/ppermute | solution.py:199
  31.6 8.8 %collective-permute-start.10 = (bf16[32,1024]{1,0:T(8,128)(2,1)S(1)}, bf16[32,1024]{1,0:T(8,128)(2,1)S(1)}, u32[]{:S(2)}, u32[]{:S(2)}) collective-permute-start(bf16[32,1024]{1,0:T(8,128)(2,1)S(1)} %get-tuple-element.27), channel_id=1, source_target_pairs={{0,3},{1,2},{2,1},{3,0},{4,7},{5,6},{6,5},{7,4},{8,12},{9,13},{10,... | collective-permute-start | bytes 196616 | tf_op jit(solution)/shard_map/ppermute | solution.py:204
  31.6 8.7 %collective-permute-start.11 = (bf16[32,1024]{1,0:T(8,128)(2,1)S(1)}, bf16[32,1024]{1,0:T(8,128)(2,1)S(1)}, u32[]{:S(2)}, u32[]{:S(2)}) collective-permute-start(bf16[32,1024]{1,0:T(8,128)(2,1)S(1)} %get-tuple-element.26), channel_id=1, source_target_pairs={{0,5},{1,4},{2,7},{3,6},{4,1},{5,0},{6,3},{7,2},{8,14},{9,15},{10,... | collective-permute-start | bytes 196616 | tf_op jit(solution)/shard_map/ppermute | solution.py:204
  33.3 8.8 %collective-permute-start.12 = (bf16[32,1024]{1,0:T(8,128)(2,1)S(1)}, bf16[32,1024]{1,0:T(8,128)(2,1)S(1)}, u32[]{:S(2)}, u32[]{:S(2)}) collective-permute-start(bf16[32,1024]{1,0:T(8,128)(2,1)S(1)} %get-tuple-element.25), channel_id=1, source_target_pairs={{0,7},{1,6},{2,5},{3,4},{4,3},{5,2},{6,1},{7,0},{8,8},{9,9},{10,10... | collective-permute-start | bytes 196616 | tf_op jit(solution)/shard_map/ppermute | solution.py:204
  38.8 4.3 %collective-permute-start.9 = (bf16[32,1024]{1,0:T(8,128)(2,1)S(1)}, bf16[32,1024]{1,0:T(8,128)(2,1)S(1)}, u32[]{:S(2)}, u32[]{:S(2)}) collective-permute-start(bf16[32,1024]{1,0:T(8,128)(2,1)S(1)} %get-tuple-element.24), channel_id=1, source_target_pairs={{0,1},{1,0},{2,3},{3,2},{4,5},{5,4},{6,7},{7,6},{8,10},{9,11},{10,... | collective-permute-start | bytes 196616 | tf_op jit(solution)/shard_map/ppermute | solution.py:204
  43.1 3.0 %copy-start.1 = (f32[128,16]{1,0:T(8,128)S(1)}, f32[128,16]{1,0:T(8,128)}, u32[]{:S(2)}) copy-start(f32[128,16]{1,0:T(8,128)} %get-tuple-element.21) | copy-start | bytes 24580
  43.1 1.4 %collective-permute-start.13 = (f32[32,1024]{1,0:T(8,128)S(1)}, f32[32,1024]{1,0:T(8,128)S(1)}, u32[]{:S(2)}, u32[]{:S(2)}) collective-permute-start(f32[32,1024]{1,0:T(8,128)S(1)} %convert_add_fusion), channel_id=1, source_target_pairs={{0,8},{1,9},{2,10},{3,11},{4,12},{5,13},{6,14},{7,15},{8,0},{9,1},... | collective-permute-start | bytes 393224 | tf_op jit(solution)/shard_map/ppermute | solution.py:206
  44.6 6.0 %collective-permute-start.14 = (f32[32,1024]{1,0:T(8,128)S(1)}, f32[32,1024]{1,0:T(8,128)S(1)}, u32[]{:S(2)}, u32[]{:S(2)}) collective-permute-start(f32[32,1024]{1,0:T(8,128)S(1)} %add.49), channel_id=1, source_target_pairs={{0,16},{1,17},{2,18},{3,19},{4,20},{5,21},{6,22},{7,23},{8,24},{9,... | collective-permute-start | bytes 393224 | tf_op jit(solution)/shard_map/ppermute | solution.py:209

commit v2 on v1

--- a/solution.py
+++ b/solution.py
@@ -17,25 +17,27 @@
 PICKS = 2
 
 
-def grads_kernel(per_head, halves, info, q_ref, do_ref, ex_ref, gate_ref, *refs):
+def grads_kernel(per_head, halves, begin_ref, lengths_ref, q_ref, do_ref, ex_ref, gate_ref, *refs):
     blocks, (mine_ref, theirs_ref, prob_ref, ds_ref, gg_ref), scratch = refs[: 2 * halves], refs[2 * halves : 2 * halves + 5], refs[2 * halves + 5 :]
     kp, vp, q4, do4, p2, ds2 = scratch
-    tokens, topk = ex_ref.shape
+    topk, tokens = ex_ref.shape
     own = blocks[0].shape[0] // 2
     total = 2 * halves * own
     pairs = kp.shape[1] // HEAD
+    begin = begin_ref[0]
+    count = lengths_ref[begin // CLEN] - begin % CLEN
     for b, ref in enumerate(blocks):
         for h in range(2 * pairs):
             rows = pl.ds((h % 2) * total + b * own, own)
             cols = pl.ds((h // 2) * HEAD, HEAD)
             kp[rows, cols] = ref[:own, h * HEAD : (h + 1) * HEAD]
             vp[rows, cols] = ref[own:, h * HEAD : (h + 1) * HEAD]
-    head = ex_ref[...] // per_head
-    pair = head // 2
-    head_t = jnp.transpose(head.astype(F32))
-    odd_t = head_t - 2.0 * jnp.floor(head_t * 0.5)
-    live = (lax.broadcasted_iota(jnp.int32, (topk, tokens), 1) < info[0]).astype(F32)
-    factor = jnp.transpose(gate_ref[...]) * live
+    head_t = jnp.floor(ex_ref[...].astype(F32) * (1.0 / per_head))
+    pair_t = jnp.floor(head_t * 0.5)
+    odd_t = head_t - 2.0 * pair_t
+    pair = jnp.transpose(pair_t)
+    live = (lax.broadcasted_iota(jnp.int32, (topk, tokens), 1) < count).astype(F32)
+    factor = gate_ref[...] * live
     gates = []
     for c in range(topk // PICKS):
         lo, hi = c * PICKS * tokens, (c + 1) * PICKS * tokens
@@ -73,7 +75,7 @@
         ds2[:total, lo:hi] = jnp.where(is_odd, 0.0, ds).astype(BF16)
         ds2[total:, lo:hi] = jnp.where(is_odd, ds, 0.0).astype(BF16)
     gg = jnp.concatenate([g[:, i * tokens : (i + 1) * tokens] for g in gates for i in range(PICKS)], axis=0)
-    gg_ref[...] = jnp.transpose(gg * live)
+    gg_ref[...] = gg * live
     for offset, (left, right, times) in enumerate(((ds2, q4, SCALE), (p2, do4, 1.0))):
         out = jnp.dot(left[...], right[...], preferred_element_type=F32) * times
         for b in range(2 * halves):
@@ -84,18 +86,16 @@
                 ref[rows, h * HEAD : (h + 1) * HEAD] = piece.astype(ref.dtype)
 
 
-def rows_kernel(per_head, halves, ex_ref, prob_ref, ds_ref, *refs):
-    blocks, (att_ref, dq_ref), (kt, vt) = refs[: 2 * halves], refs[2 * halves : 2 * halves + 2], refs[2 * halves + 2 :]
-    tokens, topk = ex_ref.shape
+def rows_kernel(per_head, halves, part, times, ex_ref, src_ref, *refs):
+    blocks, out_ref, left = refs[: 2 * halves], refs[2 * halves], refs[2 * halves + 1]
+    topk, tokens = ex_ref.shape
     own = blocks[0].shape[0] // 2
     total = 2 * halves * own
-    pairs = kt.shape[1] // total
+    pairs = left.shape[1] // total
     for h in range(2 * pairs):
-        cols = slice(h * HEAD, (h + 1) * HEAD)
-        for dst, part in ((kt, slice(0, own)), (vt, slice(own, 2 * own))):
-            whole = jnp.concatenate([ref[part, cols] for ref in blocks], axis=0)
-            dst[(h % 2) * HEAD : (h % 2 + 1) * HEAD, (h // 2) * total : (h // 2 + 1) * total] = jnp.transpose(whole)
-    head_t = jnp.transpose((ex_ref[...] // per_head).astype(F32))
+        whole = jnp.concatenate([ref[part * own : (part + 1) * own, h * HEAD : (h + 1) * HEAD] for ref in blocks], axis=0)
+        left[(h % 2) * HEAD : (h % 2 + 1) * HEAD, (h // 2) * total : (h // 2 + 1) * total] = jnp.transpose(whole)
+    head_t = jnp.floor(ex_ref[...].astype(F32) * (1.0 / per_head))
     pair_t = jnp.floor(head_t * 0.5)
     odd_t = head_t - 2.0 * pair_t
     for c in range(topk // PICKS):
@@ -104,25 +104,25 @@
         pair = jnp.concatenate([pair_t[k : k + 1, :] for k in ks], axis=1)
         is_odd = jnp.concatenate([odd_t[k : k + 1, :] for k in ks], axis=1) > 0.5
         hots = [jnp.broadcast_to(jnp.where(pair == j, 1.0, 0.0), (16, hi - lo)).astype(BF16) for j in range(pairs)]
-        for src, left, out_ref, times in ((prob_ref, vt, att_ref, None), (ds_ref, kt, dq_ref, SCALE)):
-            val = src[:, lo:hi].reshape(total // 16, 16, hi - lo)
-            wide = jnp.concatenate([(val * hot[None]).reshape(total, hi - lo) for hot in hots], axis=0)
-            out2 = jnp.dot(left[...], wide, preferred_element_type=F32)
-            out = jnp.where(is_odd, out2[HEAD:], out2[:HEAD])
-            if times is not None:
-                out = out * times
-            out = out.astype(BF16)
-            for i, k in enumerate(ks):
-                out_ref[:, k * HEAD : (k + 1) * HEAD] = jnp.transpose(out[:, i * tokens : (i + 1) * tokens])
+        val = src_ref[:, lo:hi].reshape(total // 16, 16, hi - lo)
+        wide = jnp.concatenate([(val * hot[None]).reshape(total, hi - lo) for hot in hots], axis=0)
+        out2 = jnp.dot(left[...], wide, preferred_element_type=F32)
+        out = jnp.where(is_odd, out2[HEAD:], out2[:HEAD])
+        if times is not None:
+            out = out * times
+        out = out.astype(BF16)
+        for i, k in enumerate(ks):
+            out_ref[:, k * HEAD : (k + 1) * HEAD] = jnp.transpose(out[:, i * tokens : (i + 1) * tokens])
 
 
 def gather_pairs(n_sample, n_ctx, first, second):
+    walk = list(range(0, n_ctx, 2)) + list(range(n_ctx - 1, 0, -2))
+    place = {j: i for i, j in enumerate(walk)}
     out = []
     for s in range(n_sample):
         for j in range(n_ctx):
             o = second if s % 2 else first
-            src = j ^ o if n_ctx & (n_ctx - 1) == 0 else (j + o) % n_ctx
-            out.append((s * n_ctx + src, s * n_ctx + j))
+            out.append((s * n_ctx + walk[(place[j] + o) % n_ctx], s * n_ctx + j))
     return out
 
 
@@ -143,10 +143,10 @@
     assert n_ctx % 2 == 0 and n_sample & (n_sample - 1) == 0 and n_sample > 1 and CLEN % tokens == 0
 
     begin = (lax.axis_index("sample") * n_ctx + lax.axis_index("ctx")) * tokens
-    count = lax.dynamic_index_in_dim(lengths, begin // CLEN, 0, keepdims=True) - begin % CLEN
-
-    offsets = list(range(1, n_ctx)) + [0]
-    firsts, seconds = offsets[0::2], offsets[1::2]
+
+    near_first = sorted(range(n_ctx), key=lambda o: (min(o, n_ctx - o), o))
+    firsts = (near_first[: halves - 1] + near_first[-1:])[::-1]
+    seconds = near_first[halves - 1 : -1][::-1]
     routes = [gather_pairs(n_sample, n_ctx, a, b) for a, b in zip(firsts, seconds, strict=True)]
     swap = swap_pairs(n_sample, n_ctx, 1)
     block = jnp.concatenate([prefix_keys, prefix_values], axis=0)
@@ -164,9 +164,9 @@
             jax.ShapeDtypeStruct((halves * 2 * own, width), BF16),
             jax.ShapeDtypeStruct((total, picked), BF16),
             jax.ShapeDtypeStruct((total, picked), BF16),
-            jax.ShapeDtypeStruct((tokens, topk), F32),
+            jax.ShapeDtypeStruct((topk, tokens), F32),
         ),
-        in_specs=[smem] + [vmem] * (4 + 2 * halves),
+        in_specs=[smem] * 2 + [vmem] * (4 + 2 * halves),
         out_specs=[vmem] * 5,
         scratch_shapes=[
             pltpu.VMEM((2 * total, pairs * HEAD), BF16),
@@ -178,23 +178,21 @@
         ],
         cost_estimate=pl.CostEstimate(flops=flops, bytes_accessed=4 << 20, transcendentals=picked * total),
         name="grads",
-    )(count, queries, d_out, experts, gate, *blocks)
-
-    attended, query_grad = pl.pallas_call(
-        functools.partial(rows_kernel, per_head, halves),
-        out_shape=(
-            jax.ShapeDtypeStruct(queries.shape, BF16),
-            jax.ShapeDtypeStruct(queries.shape, BF16),
-        ),
-        in_specs=[vmem] * (3 + 2 * halves),
-        out_specs=[vmem] * 2,
-        scratch_shapes=[
-            pltpu.VMEM((2 * HEAD, pairs * total), BF16),
-            pltpu.VMEM((2 * HEAD, pairs * total), BF16),
-        ],
-        cost_estimate=pl.CostEstimate(flops=flops // 2, bytes_accessed=2 << 20, transcendentals=0),
-        name="rows",
-    )(experts, prob, ds, *blocks)
+    )(begin.reshape(1), lengths, queries, d_out, experts.T, gate.T, *blocks)
+
+    def rows(part, times, src, name):
+        return pl.pallas_call(
+            functools.partial(rows_kernel, per_head, halves, part, times),
+            out_shape=jax.ShapeDtypeStruct(queries.shape, BF16),
+            in_specs=[vmem] * (2 + 2 * halves),
+            out_specs=vmem,
+            scratch_shapes=[pltpu.VMEM((2 * HEAD, pairs * total), BF16)],
+            cost_estimate=pl.CostEstimate(flops=flops // 4, bytes_accessed=2 << 20, transcendentals=0),
+            name=name,
+        )(experts.T, src, *blocks)
+
+    attended = rows(1, None, prob, "attended")
+    query_grad = rows(0, SCALE, ds, "query_grad")
 
     from_other = lax.ppermute(theirs, AXES, swap).astype(F32)
     parts = []
@@ -208,7 +206,7 @@
     while bit < n_sample:
         share = share + lax.ppermute(share, AXES, swap_pairs(n_sample, n_ctx, bit))
         bit *= 2
-    return (attended, query_grad, gate_grad, share[:own], share[own:])
+    return (attended, query_grad, gate_grad.T, share[:own], share[own:])
 
 
 def solution(mesh):

time: 51.6 us -> 44.4 us (0.86)
  waiting for transfers between devices: 11.8 us -> 6.11 us
  local copies, waits for them, and re-layouts: 6.77 us -> 2.03 us
  starting transfers between devices: 21.5 us -> 23.8 us
  Pallas kernels: 9.46 us -> 11.3 us
  between operations: 1.5 us -> 0.78 us
    ppermute x4, waiting for transfers between devices: 6.32 us -> 0.15 us  [local(): got = [lax.ppermute(block, AXES, r) for r in routes]]
    ppermute x4, starting transfers between devices: 0.56 us -> 5.1 us  [local(): other = [lax.ppermute(g, AXES, swap) for g in got]]
    unnamed x32 -> x21, local copies, waits for them, and re-layouts: 5.53 us -> 1.37 us
    ppermute x4, starting transfers between devices: 8.77 us -> 5.84 us  [local(): lax.ppermute((mine[rows] + from_other[rows]).astype(BF16), AXES, back)]
    ppermute x1, starting transfers between devices: 0.07 us -> 2.07 us  [local(): share = share + lax.ppermute(share, AXES, swap)]
    pallas_call x1 -> x2, Pallas kernels: 3.74 us -> 5.53 us  [rows(): pl.pallas_call(functools.partial(rows_kernel, per_head, halves, part, tim...]
    ppermute x4, starting transfers between devices: 10 us -> 8.78 us  [local(): got = [lax.ppermute(block, AXES, r) for r in routes]]
    ppermute x4, waiting for transfers between devices: 0.01 us -> 0.87 us  [local(): other = [lax.ppermute(g, AXES, swap) for g in got]]
  transfers between devices with their start and end apart: 15 -> 15, of which waited for: 6 -> 7; matrix products, arithmetic and copies ran while one was open for 5% -> 0% of each run, Pallas kernels for 7% -> 13%
where the time goes in v2:
time: 44.4 us; the launch traced here: 44.2 us
  starting transfers between devices  23.8 us (54%)
  Pallas kernels  11.3 us (25%)
  waiting for transfers between devices  6.11 us (14%)
  local copies, waits for them, and re-layouts  2.03 us (5%)
  between operations  0.78 us (2%)
    ppermute x4, starting transfers between devices, local(): got = [lax.ppermute(block, AXES, r) for r in routes]  8.78 us
    ppermute x4, starting transfers between devices, local(): lax.ppermute((mine[rows] + from_other[rows]).astype(BF16), AXES, back)  5.84 us
    pallas_call x1, Pallas kernels, local(): pl.pallas_call(functools.partial(grads_kernel, per_head, halves), out_sha...  5.78 us
    pallas_call x2, Pallas kernels, rows(): pl.pallas_call(functools.partial(rows_kernel, per_head, halves, part, tim...  5.53 us
    ppermute x4, starting transfers between devices, local(): other = [lax.ppermute(g, AXES, swap) for g in got]  5.1 us
    ppermute x4, waiting for transfers between devices, local(): lax.ppermute((mine[rows] + from_other[rows]).astype(BF16), AXES, back)  2.71 us
    ppermute x1, starting transfers between devices, local(): share = share + lax.ppermute(share, AXES, swap)  2.07 us
    ppermute x1, starting transfers between devices, local(): share = share + lax.ppermute(share, AXES, swap_pairs(n_sample, n_ctx, bit))  1.55 us
  transfers between devices with their start and end apart: 15, of which 7 were waited for; matrix products, arithmetic and copies ran while one was open for 0% of the time, Pallas kernels for 13%

profile of v2, /device:TPU:0, one launch (start us, length us, event | category | flops | bytes accessed | tf_op | source)
XLA Modules:
  0.0 44.2 jit_solution(7849088465072928174)
XLA Ops:
  0.6 0.0 copy-start.1
  0.6 0.8 %constant_dynamic-update-slice_fusion.1 = bf16[32,1024]{1,0:T(8,128)(2,1)S(1)} fusion(bf16[16,1024]{1,0:T(8,128)(2,1)} %param.10), kind=kLoop, calls=%fused_computation.10 | loop fusion | bytes 65536
  1.4 0.0 copy-done.1
  1.4 0.7 %collective-permute-start.3 = (bf16[32,1024]{1,0:T(8,128)(2,1)S(1)}, bf16[32,1024]{1,0:T(8,128)(2,1)S(1)}, u32[]{:S(2)}, u32[]{:S(2)}) collective-permute-start(bf16[32,1024]{1,0:T(8,128)(2,1)S(1)} %constant_dynamic-update-slice_fusion), channel_id=1, source_target_pairs={{0,0},{1,1},{2,2},{3,3},{4,4},{5,5},{6,6},{7,7},{12,8},{10,9},{14,... | collective-permute-start | bytes 196616 | tf_op jit(solution)/shard_map/ppermute | solution.py:153
  2.1 3.0 %collective-permute-start.2 = (bf16[32,1024]{1,0:T(8,128)(2,1)S(1)}, bf16[32,1024]{1,0:T(8,128)(2,1)S(1)}, u32[]{:S(2)}, u32[]{:S(2)}) collective-permute-start(bf16[32,1024]{1,0:T(8,128)(2,1)S(1)} %constant_dynamic-update-slice_fusion), channel_id=1, source_target_pairs={{2,0},{0,1},{4,2},{1,3},{6,4},{3,5},{7,6},{5,7},{11,8},{13,9},{9,1... | collective-permute-start | bytes 196616 | tf_op jit(solution)/shard_map/ppermute | solution.py:153
  5.1 0.1 collective-permute-start.1
  5.3 4.9 %collective-permute-start = (bf16[32,1024]{1,0:T(8,128)(2,1)S(1)}, bf16[32,1024]{1,0:T(8,128)(2,1)S(1)}, u32[]{:S(2)}, u32[]{:S(2)}) collective-permute-start(bf16[32,1024]{1,0:T(8,128)(2,1)S(1)} %constant_dynamic-update-slice_fusion), channel_id=1, source_target_pairs={{7,0},{6,1},{5,2},{4,3},{3,4},{2,5},{1,6},{0,7},{13,8},{15,9},{11,... | collective-permute-start | bytes 196616 | tf_op jit(solution)/shard_map/ppermute | solution.py:153
  10.2 0.0 collective-permute-done.3.refs_3_
  10.2 0.0 copy-start.2
  10.2 0.2 collective-permute-start.7
  10.4 0.0 collective-permute-done.2.refs_2_
  10.4 0.0 copy-start.3
  10.4 0.6 %collective-permute-start.6 = (bf16[32,1024]{1,0:T(8,128)(2,1)S(1)}, bf16[32,1024]{1,0:T(8,128)(2,1)S(1)}, u32[]{:S(2)}, u32[]{:S(2)}) collective-permute-start(bf16[32,1024]{1,0:T(8,128)(2,1)S(1)} %collective-permute-done.2.refs_2_), channel_id=1, source_target_pairs={{0,8},{1,9},{2,10},{3,11},{4,12},{5,13},{6,14},{7,15},{8,0},{9,1},... | collective-permute-start | bytes 196616 | tf_op jit(solution)/shard_map/ppermute | solution.py:154
  11.0 0.0 collective-permute-done.1.refs_1_
  11.0 0.0 copy-start.4
  11.0 2.8 %collective-permute-start.5 = (bf16[32,1024]{1,0:T(8,128)(2,1)S(1)}, bf16[32,1024]{1,0:T(8,128)(2,1)S(1)}, u32[]{:S(2)}, u32[]{:S(2)}) collective-permute-start(bf16[32,1024]{1,0:T(8,128)(2,1)S(1)} %collective-permute-done.1.refs_1_), channel_id=1, source_target_pairs={{0,8},{1,9},{2,10},{3,11},{4,12},{5,13},{6,14},{7,15},{8,0},{9,1},... | collective-permute-start | bytes 196616 | tf_op jit(solution)/shard_map/ppermute | solution.py:154
  13.8 0.1 collective-permute-done.refs_0_
  13.9 0.0 copy-start.5
  13.9 1.5 %collective-permute-start.4 = (bf16[32,1024]{1,0:T(8,128)(2,1)S(1)}, bf16[32,1024]{1,0:T(8,128)(2,1)S(1)}, u32[]{:S(2)}, u32[]{:S(2)}) collective-permute-start(bf16[32,1024]{1,0:T(8,128)(2,1)S(1)} %collective-permute-done.refs_0_), channel_id=1, source_target_pairs={{0,8},{1,9},{2,10},{3,11},{4,12},{5,13},{6,14},{7,15},{8,0},{9,1},... | collective-permute-start | bytes 196616 | tf_op jit(solution)/shard_map/ppermute | solution.py:154
  15.5 0.0 collective-permute-done.7.refs_7_
  15.5 0.0 copy-start.6
  15.5 0.0 collective-permute-done.6.refs_6_
  15.5 0.0 copy-start.7
  15.5 0.0 collective-permute-done.5.refs_5_
  15.5 0.0 copy-start.8
  15.5 0.9 %collective-permute-done.4.refs_4_ = bf16[32,1024]{1,0:T(8,128)(2,1)S(1)} collective-permute-done((bf16[32,1024]{1,0:T(8,128)(2,1)S(1)}, bf16[32,1024]{1,0:T(8,128)(2,1)S(1)}, u32[]{:S(2)}, u32[]{:S(2)}) %collective-permute-start.4) | collective-permute-done | bytes 65568 | tf_op jit(solution)/shard_map/ppermute | solution.py:154
  16.4 0.0 copy-start.9
  16.4 0.0 copy-done.2
  16.4 0.0 copy-done.3
  16.4 0.0 copy-done.4
  16.4 0.0 copy-done.5
  16.4 0.0 copy-done.6
  16.4 0.0 copy-done.7
  16.4 0.0 copy-done.8
  16.4 0.6 %copy-done.9 = bf16[32,1024]{1,0:T(8,128)(2,1)} copy-done((bf16[32,1024]{1,0:T(8,128)(2,1)}, bf16[32,1024]{1,0:T(8,128)(2,1)S(1)}, u32[]{:S(2)}) %copy-start.9) | copy-done | bytes 65560
  17.0 5.8 %grads.1 = (f32[128,1024]{1,0:T(8,128)}, bf16[128,1024]{1,0:T(8,128)(2,1)}, bf16[128,2048]{1,0:T(8,128)(2,1)}, bf16[128,2048]{1,0:T(8,128)(2,1)}, f32[16,128]{1,0:T(8,128)}) custom-call(s32[1]{0:T(128)} %bitcast.1.begin_ref, s32[4]{0:T(128)} %lengths_ref.1, bf16[128,2048]{1,0:T(8,128)(2,1)} %q_ref.1, bf16[128,2048]{1,0:T(8,128)(2,1)} %do_ref.1, ...), custom_call_target="tpu_custom_call" | custom-call | flops 2147483648 | bytes 4194304 | tf_op jit(solution)/shard_map/grads/pallas_call | solution.py:160
  22.8 0.0 copy-start
  22.8 0.4 collective-permute-start.8
  23.2 1.4 %collective-permute-done.8 = bf16[128,1024]{1,0:T(8,128)(2,1)S(1)} collective-permute-done((bf16[128,1024]{1,0:T(8,128)(2,1)}, bf16[128,1024]{1,0:T(8,128)(2,1)S(1)}, u32[]{:S(2)}, u32[]{:S(2)}) %collective-permute-start.8) | collective-permute-done | bytes 262176 | tf_op jit(solution)/shard_map/ppermute | solution.py:197
  24.6 0.0 copy-done
  24.6 0.1 fusion.3
  24.7 3.1 %collective-permute-start.9 = (bf16[32,1024]{1,0:T(8,128)(2,1)S(1)}, bf16[32,1024]{1,0:T(8,128)(2,1)S(1)}, u32[]{:S(2)}, u32[]{:S(2)}) collective-permute-start(bf16[32,1024]{1,0:T(8,128)(2,1)S(1)} %get-tuple-element.15), channel_id=1, source_target_pairs={{0,7},{1,6},{2,5},{3,4},{4,3},{5,2},{6,1},{7,0},{8,13},{9,15},{10,... | collective-permute-start | bytes 196616 | tf_op jit(solution)/shard_map/ppermute | solution.py:202
  27.8 0.7 %collective-permute-start.12 = (bf16[32,1024]{1,0:T(8,128)(2,1)S(1)}, bf16[32,1024]{1,0:T(8,128)(2,1)S(1)}, u32[]{:S(2)}, u32[]{:S(2)}) collective-permute-start(bf16[32,1024]{1,0:T(8,128)(2,1)S(1)} %get-tuple-element.16), channel_id=1, source_target_pairs={{0,0},{1,1},{2,2},{3,3},{4,4},{5,5},{6,6},{7,7},{8,12},{9,10},{10,... | collective-permute-start | bytes 196616 | tf_op jit(solution)/shard_map/ppermute | solution.py:202
  28.5 0.1 collective-permute-start.11
  28.5 2.0 %collective-permute-start.10 = (bf16[32,1024]{1,0:T(8,128)(2,1)S(1)}, bf16[32,1024]{1,0:T(8,128)(2,1)S(1)}, u32[]{:S(2)}, u32[]{:S(2)}) collective-permute-start(bf16[32,1024]{1,0:T(8,128)(2,1)S(1)} %get-tuple-element.18), channel_id=1, source_target_pairs={{0,1},{1,3},{2,0},{3,5},{4,2},{5,7},{6,4},{7,6},{8,14},{9,12},{10,... | collective-permute-start | bytes 196616 | tf_op jit(solution)/shard_map/ppermute | solution.py:202
  30.6 1.2 %collective-permute-done.9 = bf16[32,1024]{1,0:T(8,128)(2,1)S(1)} collective-permute-done((bf16[32,1024]{1,0:T(8,128)(2,1)S(1)}, bf16[32,1024]{1,0:T(8,128)(2,1)S(1)}, u32[]{:S(2)}, u32[]{:S(2)}) %collective-permute-start.9) | collective-permute-done | bytes 65568 | tf_op jit(solution)/shard_map/ppermute | solution.py:202
  31.8 0.0 collective-permute-done.12
  31.8 1.4 %collective-permute-done.11 = bf16[32,1024]{1,0:T(8,128)(2,1)S(1)} collective-permute-done((bf16[32,1024]{1,0:T(8,128)(2,1)S(1)}, bf16[32,1024]{1,0:T(8,128)(2,1)S(1)}, u32[]{:S(2)}, u32[]{:S(2)}) %collective-permute-start.11) | collective-permute-done | bytes 65568 | tf_op jit(solution)/shard_map/ppermute | solution.py:202
  33.2 0.1 collective-permute-done.10
  33.3 2.1 %collective-permute-start.13 = (f32[32,1024]{1,0:T(8,128)S(1)}, f32[32,1024]{1,0:T(8,128)S(1)}, u32[]{:S(2)}, u32[]{:S(2)}) collective-permute-start(f32[32,1024]{1,0:T(8,128)S(1)} %convert_add_fusion), channel_id=1, source_target_pairs={{0,8},{1,9},{2,10},{3,11},{4,12},{5,13},{6,14},{7,15},{8,0},{9,1},... | collective-permute-start | bytes 393224 | tf_op jit(solution)/shard_map/ppermute | solution.py:204
  35.4 1.0 %collective-permute-done.13 = f32[32,1024]{1,0:T(8,128)S(1)} collective-permute-done((f32[32,1024]{1,0:T(8,128)S(1)}, f32[32,1024]{1,0:T(8,128)S(1)}, u32[]{:S(2)}, u32[]{:S(2)}) %collective-permute-start.13) | collective-permute-done | bytes 131104 | tf_op jit(solution)/shard_map/ppermute | solution.py:204
  36.4 1.6 %collective-permute-start.14 = (f32[32,1024]{1,0:T(8,128)S(1)}, f32[32,1024]{1,0:T(8,128)S(1)}, u32[]{:S(2)}, u32[]{:S(2)}) collective-permute-start(f32[32,1024]{1,0:T(8,128)S(1)} %add.38), channel_id=1, source_target_pairs={{0,16},{1,17},{2,18},{3,19},{4,20},{5,21},{6,22},{7,23},{8,24},{9,... | collective-permute-start | bytes 393224 | tf_op jit(solution)/shard_map/ppermute | solution.py:207
  37.9 2.8 %attended.1 = bf16[128,2048]{1,0:T(8,128)(2,1)} custom-call(s32[16,128]{1,0:T(8,128)} %bitcast.6, bf16[128,2048]{1,0:T(8,128)(2,1)} %get-tuple-element.10.src_ref, bf16[32,1024]{1,0:T(8,128)(2,1)} %copy-done.5, bf16[32,1024]{1,0:T(8,128)(2,1)} %copy-done.4, bf16[32,1024]{1,0:T(8,128)(2,1)} %copy-done.3, bf16[32,1024]{1,0:T(8,128)(2,1)} %copy-done.2, ...), custom_call_target="tpu_custom_call" | custom-call | flops 536870912 | bytes 2097152 | tf_op jit(solution)/shard_map/attended/pallas_call | solution.py:184
  40.7 2.8 %query_grad.1 = bf16[128,2048]{1,0:T(8,128)(2,1)} custom-call(s32[16,128]{1,0:T(8,128)} %bitcast.7, bf16[128,2048]{1,0:T(8,128)(2,1)} %get-tuple-element.11.src_ref, bf16[32,1024]{1,0:T(8,128)(2,1)} %copy-done.5, bf16[32,1024]{1,0:T(8,128)(2,1)} %copy-done.4, bf16[32,1024]{1,0:T(8,128)(2,1)} %copy-done.3, bf16[32,1024]{1,0:T(8,128)(2,1)} %copy-done.2, ...), custom_call_target="tpu_custom_call" | custom-call | flops 536870912 | bytes 2097152 | tf_op jit(solution)/shard_map/query_grad/pallas_call | solution.py:184
  43.5 0.0 collective-permute-done.14
  43.5 0.7 %fusion.4 = (f32[16,1024]{1,0:T(8,128)}, f32[16,1024]{1,0:T(8,128)}) fusion(f32[32,1024]{1,0:T(8,128)S(1)} %add.39), kind=kLoop, calls=%fused_computation.11 | loop fusion | bytes 262144 | tf_op jit(solution)/shard_map/slice | solution.py:209
  (5 shorter events, 0.1 us)
Async XLA Ops:
  0.6 0.8 %copy-start.1 = (bf16[16,1024]{1,0:T(8,128)(2,1)S(1)}, bf16[16,1024]{1,0:T(8,128)(2,1)}, u32[]{:S(2)}) copy-start(bf16[16,1024]{1,0:T(8,128)(2,1)} %param.11) | copy-start | bytes 98308
  1.4 8.8 %collective-permute-start.3 = (bf16[32,1024]{1,0:T(8,128)(2,1)S(1)}, bf16[32,1024]{1,0:T(8,128)(2,1)S(1)}, u32[]{:S(2)}, u32[]{:S(2)}) collective-permute-start(bf16[32,1024]{1,0:T(8,128)(2,1)S(1)} %constant_dynamic-update-slice_fusion), channel_id=1, source_target_pairs={{0,0},{1,1},{2,2},{3,3},{4,4},{5,5},{6,6},{7,7},{12,8},{10,9},{14,... | collective-permute-start | bytes 196616 | tf_op jit(solution)/shard_map/ppermute | solution.py:153
  2.1 8.3 %collective-permute-start.2 = (bf16[32,1024]{1,0:T(8,128)(2,1)S(1)}, bf16[32,1024]{1,0:T(8,128)(2,1)S(1)}, u32[]{:S(2)}, u32[]{:S(2)}) collective-permute-start(bf16[32,1024]{1,0:T(8,128)(2,1)S(1)} %constant_dynamic-update-slice_fusion), channel_id=1, source_target_pairs={{2,0},{0,1},{4,2},{1,3},{6,4},{3,5},{7,6},{5,7},{11,8},{13,9},{9,1... | collective-permute-start | bytes 196616 | tf_op jit(solution)/shard_map/ppermute | solution.py:153
  5.1 5.8 %collective-permute-start.1 = (bf16[32,1024]{1,0:T(8,128)(2,1)S(1)}, bf16[32,1024]{1,0:T(8,128)(2,1)S(1)}, u32[]{:S(2)}, u32[]{:S(2)}) collective-permute-start(bf16[32,1024]{1,0:T(8,128)(2,1)S(1)} %constant_dynamic-update-slice_fusion), channel_id=1, source_target_pairs={{1,0},{3,1},{0,2},{5,3},{2,4},{7,5},{4,6},{6,7},{14,8},{12,9},{15,... | collective-permute-start | bytes 196616 | tf_op jit(solution)/shard_map/ppermute | solution.py:153
  5.3 8.7 %collective-permute-start = (bf16[32,1024]{1,0:T(8,128)(2,1)S(1)}, bf16[32,1024]{1,0:T(8,128)(2,1)S(1)}, u32[]{:S(2)}, u32[]{:S(2)}) collective-permute-start(bf16[32,1024]{1,0:T(8,128)(2,1)S(1)} %constant_dynamic-update-slice_fusion), channel_id=1, source_target_pairs={{7,0},{6,1},{5,2},{4,3},{3,4},{2,5},{1,6},{0,7},{13,8},{15,9},{11,... | collective-permute-start | bytes 196616 | tf_op jit(solution)/shard_map/ppermute | solution.py:153
  10.2 6.2 %copy-start.2 = (bf16[32,1024]{1,0:T(8,128)(2,1)}, bf16[32,1024]{1,0:T(8,128)(2,1)S(1)}, u32[]{:S(2)}) copy-start(bf16[32,1024]{1,0:T(8,128)(2,1)S(1)} %collective-permute-done.3.refs_3_) | copy-start | bytes 196612
  10.2 5.3 %collective-permute-start.7 = (bf16[32,1024]{1,0:T(8,128)(2,1)S(1)}, bf16[32,1024]{1,0:T(8,128)(2,1)S(1)}, u32[]{:S(2)}, u32[]{:S(2)}) collective-permute-start(bf16[32,1024]{1,0:T(8,128)(2,1)S(1)} %collective-permute-done.3.refs_3_), channel_id=1, source_target_pairs={{0,8},{1,9},{2,10},{3,11},{4,12},{5,13},{6,14},{7,15},{8,0},{9,1},... | collective-permute-start | bytes 196616 | tf_op jit(solution)/shard_map/ppermute | solution.py:154
  10.4 6.0 %copy-start.3 = (bf16[32,1024]{1,0:T(8,128)(2,1)}, bf16[32,1024]{1,0:T(8,128)(2,1)S(1)}, u32[]{:S(2)}) copy-start(bf16[32,1024]{1,0:T(8,128)(2,1)S(1)} %collective-permute-done.2.refs_2_) | copy-start | bytes 196612
  10.4 5.1 %collective-permute-start.6 = (bf16[32,1024]{1,0:T(8,128)(2,1)S(1)}, bf16[32,1024]{1,0:T(8,128)(2,1)S(1)}, u32[]{:S(2)}, u32[]{:S(2)}) collective-permute-start(bf16[32,1024]{1,0:T(8,128)(2,1)S(1)} %collective-permute-done.2.refs_2_), channel_id=1, source_target_pairs={{0,8},{1,9},{2,10},{3,11},{4,12},{5,13},{6,14},{7,15},{8,0},{9,1},... | collective-permute-start | bytes 196616 | tf_op jit(solution)/shard_map/ppermute | solution.py:154
  11.0 5.4 %copy-start.4 = (bf16[32,1024]{1,0:T(8,128)(2,1)}, bf16[32,1024]{1,0:T(8,128)(2,1)S(1)}, u32[]{:S(2)}) copy-start(bf16[32,1024]{1,0:T(8,128)(2,1)S(1)} %collective-permute-done.1.refs_1_) | copy-start | bytes 196612
  11.0 4.5 %collective-permute-start.5 = (bf16[32,1024]{1,0:T(8,128)(2,1)S(1)}, bf16[32,1024]{1,0:T(8,128)(2,1)S(1)}, u32[]{:S(2)}, u32[]{:S(2)}) collective-permute-start(bf16[32,1024]{1,0:T(8,128)(2,1)S(1)} %collective-permute-done.1.refs_1_), channel_id=1, source_target_pairs={{0,8},{1,9},{2,10},{3,11},{4,12},{5,13},{6,14},{7,15},{8,0},{9,1},... | collective-permute-start | bytes 196616 | tf_op jit(solution)/shard_map/ppermute | solution.py:154
  13.9 2.5 %copy-start.5 = (bf16[32,1024]{1,0:T(8,128)(2,1)}, bf16[32,1024]{1,0:T(8,128)(2,1)S(1)}, u32[]{:S(2)}) copy-start(bf16[32,1024]{1,0:T(8,128)(2,1)S(1)} %collective-permute-done.refs_0_) | copy-start | bytes 196612
  13.9 2.4 %collective-permute-start.4 = (bf16[32,1024]{1,0:T(8,128)(2,1)S(1)}, bf16[32,1024]{1,0:T(8,128)(2,1)S(1)}, u32[]{:S(2)}, u32[]{:S(2)}) collective-permute-start(bf16[32,1024]{1,0:T(8,128)(2,1)S(1)} %collective-permute-done.refs_0_), channel_id=1, source_target_pairs={{0,8},{1,9},{2,10},{3,11},{4,12},{5,13},{6,14},{7,15},{8,0},{9,1},... | collective-permute-start | bytes 196616 | tf_op jit(solution)/shard_map/ppermute | solution.py:154
  15.5 0.9 %copy-start.6 = (bf16[32,1024]{1,0:T(8,128)(2,1)}, bf16[32,1024]{1,0:T(8,128)(2,1)S(1)}, u32[]{:S(2)}) copy-start(bf16[32,1024]{1,0:T(8,128)(2,1)S(1)} %collective-permute-done.7.refs_7_) | copy-start | bytes 196612
  15.5 0.9 %copy-start.7 = (bf16[32,1024]{1,0:T(8,128)(2,1)}, bf16[32,1024]{1,0:T(8,128)(2,1)S(1)}, u32[]{:S(2)}) copy-start(bf16[32,1024]{1,0:T(8,128)(2,1)S(1)} %collective-permute-done.6.refs_6_) | copy-start | bytes 196612
  15.5 0.9 %copy-start.8 = (bf16[32,1024]{1,0:T(8,128)(2,1)}, bf16[32,1024]{1,0:T(8,128)(2,1)S(1)}, u32[]{:S(2)}) copy-start(bf16[32,1024]{1,0:T(8,128)(2,1)S(1)} %collective-permute-done.5.refs_5_) | copy-start | bytes 196612
  16.4 0.6 %copy-start.9 = (bf16[32,1024]{1,0:T(8,128)(2,1)}, bf16[32,1024]{1,0:T(8,128)(2,1)S(1)}, u32[]{:S(2)}) copy-start(bf16[32,1024]{1,0:T(8,128)(2,1)S(1)} %collective-permute-done.4.refs_4_) | copy-start | bytes 196612
  22.8 1.9 %copy-start = (f32[128,1024]{1,0:T(8,128)S(1)}, f32[128,1024]{1,0:T(8,128)}, u32[]{:S(2)}) copy-start(f32[128,1024]{1,0:T(8,128)} %get-tuple-element.13) | copy-start | bytes 1572868
  22.8 1.8 %collective-permute-start.8 = (bf16[128,1024]{1,0:T(8,128)(2,1)}, bf16[128,1024]{1,0:T(8,128)(2,1)S(1)}, u32[]{:S(2)}, u32[]{:S(2)}) collective-permute-start(bf16[128,1024]{1,0:T(8,128)(2,1)} %get-tuple-element.14), channel_id=1, source_target_pairs={{0,8},{1,9},{2,10},{3,11},{4,12},{5,13},{6,14},{7,15},{8,0},{9,1},... | collective-permute-start | bytes 786440 | tf_op jit(solution)/shard_map/ppermute | solution.py:197
  24.7 7.1 %collective-permute-start.9 = (bf16[32,1024]{1,0:T(8,128)(2,1)S(1)}, bf16[32,1024]{1,0:T(8,128)(2,1)S(1)}, u32[]{:S(2)}, u32[]{:S(2)}) collective-permute-start(bf16[32,1024]{1,0:T(8,128)(2,1)S(1)} %get-tuple-element.15), channel_id=1, source_target_pairs={{0,7},{1,6},{2,5},{3,4},{4,3},{5,2},{6,1},{7,0},{8,13},{9,15},{10,... | collective-permute-start | bytes 196616 | tf_op jit(solution)/shard_map/ppermute | solution.py:202
  27.8 4.0 %collective-permute-start.12 = (bf16[32,1024]{1,0:T(8,128)(2,1)S(1)}, bf16[32,1024]{1,0:T(8,128)(2,1)S(1)}, u32[]{:S(2)}, u32[]{:S(2)}) collective-permute-start(bf16[32,1024]{1,0:T(8,128)(2,1)S(1)} %get-tuple-element.16), channel_id=1, source_target_pairs={{0,0},{1,1},{2,2},{3,3},{4,4},{5,5},{6,6},{7,7},{8,12},{9,10},{10,... | collective-permute-start | bytes 196616 | tf_op jit(solution)/shard_map/ppermute | solution.py:202
  28.5 4.7 %collective-permute-start.11 = (bf16[32,1024]{1,0:T(8,128)(2,1)S(1)}, bf16[32,1024]{1,0:T(8,128)(2,1)S(1)}, u32[]{:S(2)}, u32[]{:S(2)}) collective-permute-start(bf16[32,1024]{1,0:T(8,128)(2,1)S(1)} %get-tuple-element.17), channel_id=1, source_target_pairs={{0,2},{1,0},{2,4},{3,1},{4,6},{5,3},{6,7},{7,5},{8,11},{9,13},{10,... | collective-permute-start | bytes 196616 | tf_op jit(solution)/shard_map/ppermute | solution.py:202
  28.5 4.7 %collective-permute-start.10 = (bf16[32,1024]{1,0:T(8,128)(2,1)S(1)}, bf16[32,1024]{1,0:T(8,128)(2,1)S(1)}, u32[]{:S(2)}, u32[]{:S(2)}) collective-permute-start(bf16[32,1024]{1,0:T(8,128)(2,1)S(1)} %get-tuple-element.18), channel_id=1, source_target_pairs={{0,1},{1,3},{2,0},{3,5},{4,2},{5,7},{6,4},{7,6},{8,14},{9,12},{10,... | collective-permute-start | bytes 196616 | tf_op jit(solution)/shard_map/ppermute | solution.py:202
  33.3 3.1 %collective-permute-start.13 = (f32[32,1024]{1,0:T(8,128)S(1)}, f32[32,1024]{1,0:T(8,128)S(1)}, u32[]{:S(2)}, u32[]{:S(2)}) collective-permute-start(f32[32,1024]{1,0:T(8,128)S(1)} %convert_add_fusion), channel_id=1, source_target_pairs={{0,8},{1,9},{2,10},{3,11},{4,12},{5,13},{6,14},{7,15},{8,0},{9,1},... | collective-permute-start | bytes 393224 | tf_op jit(solution)/shard_map/ppermute | solution.py:204
  36.4 7.1 %collective-permute-start.14 = (f32[32,1024]{1,0:T(8,128)S(1)}, f32[32,1024]{1,0:T(8,128)S(1)}, u32[]{:S(2)}, u32[]{:S(2)}) collective-permute-start(f32[32,1024]{1,0:T(8,128)S(1)} %add.38), channel_id=1, source_target_pairs={{0,16},{1,17},{2,18},{3,19},{4,20},{5,21},{6,22},{7,23},{8,24},{9,... | collective-permute-start | bytes 393224 | tf_op jit(solution)/shard_map/ppermute | solution.py:207
